TPU v7x, 32 devices: a whole 2x2x4 slice. The times are simulated.
32 devices in a mesh: dp: 2 (over x), win: 4 (over y, core), tensor: 4 (over z).
Axes of the slice: x: 2, y: 2, z: 4, core: 2. Of those that a mesh axis runs over, the one named last changes fastest.
Arguments:
- tokens: bfloat16 [2, 12, 588, 768], P('dp', 'win', 'tensor'), may hold values from -6 to 6
- window_ids: int32 [2, 12, 3], P('dp', 'win'), may hold values from 0 to 25, as said below
- norm1_gain: bfloat16 [768], replicated, may hold values from 0.5 to 1.5
- norm1_bias: bfloat16 [768], replicated, may hold values from -1.75 to 1.75
- qkv_weight: bfloat16 [768, 3, 768], P(('dp', 'win'), None, 'tensor'), may hold values from -0.21875 to 0.21875
- qv_bias: bfloat16 [2, 768], P(None, 'tensor'), may hold values from -3 to 3
- rel_height: bfloat16 [27, 64], replicated, may hold values from -0.875 to 0.875
- rel_width: bfloat16 [27, 64], replicated, may hold values from -0.875 to 0.875
- proj_weight: bfloat16 [768, 768], P('tensor', ('dp', 'win')), may hold values from -0.875 to 0.875
- proj_bias: bfloat16 [768], replicated, may hold values from -1.75 to 1.75
- norm2_gain: bfloat16 [768], replicated, may hold values from 0.5 to 1.5
- norm2_bias: bfloat16 [768], replicated, may hold values from -1.75 to 1.75
- fc1_weight: bfloat16 [768, 3072], P(('dp', 'win'), 'tensor'), may hold values from -0.21875 to 0.21875
- fc1_bias: bfloat16 [3072], P('tensor'), may hold values from -3 to 3
- fc2_weight: bfloat16 [3072, 768], P('tensor', ('dp', 'win')), may hold values from -0.109375 to 0.109375
- fc2_bias: bfloat16 [768], replicated, may hold values from -1.75 to 1.75
- out_grad: bfloat16 [2, 12, 588, 768], P('dp', 'win', 'tensor'), may hold values from -6 to 6
Outputs:
- output: bfloat16 [2, 12, 588, 768], P('dp', 'win', 'tensor')
- grad_tokens: float32 [2, 12, 588, 768], P('dp', 'win', 'tensor')
- grad_norm1_gain: float32 [768], replicated
- grad_norm1_bias: float32 [768], replicated
- grad_qkv_weight: float32 [768, 3, 768], P(('dp', 'win'), None, 'tensor')
- grad_qv_bias: float32 [2, 768], replicated
- grad_rel_height: float32 [27, 64], replicated
- grad_rel_width: float32 [27, 64], replicated
- grad_proj_weight: float32 [768, 768], P('tensor', ('dp', 'win'))
- grad_proj_bias: float32 [768], replicated
- grad_norm2_gain: float32 [768], replicated
- grad_norm2_bias: float32 [768], replicated
- grad_fc1_weight: float32 [768, 3072], P(('dp', 'win'), 'tensor')
- grad_fc1_bias: float32 [3072], replicated
- grad_fc2_weight: float32 [3072, 768], P('tensor', ('dp', 'win'))
- grad_fc2_bias: float32 [768], replicated
Inputs may be any that keep to these rules, and one draw needn't show every extreme that they name: `window_ids`: every window 0 to 24 of an image stands in exactly one slot of that image, the value 25 marks an empty slot, and in every image one index of win holds 9 windows.
All inputs are finite; a program needn't handle non-finite values.
Results may differ from a plain program's by a relative error of at most 0.015.
Values may be sent and summed in bfloat16 or wider, within the bound.
A program may use at most 128 MiB of HBM per device.

v0:
```python
from functools import partial
import math

import jax
import jax.numpy as jnp
from jax import lax
from jax.sharding import PartitionSpec as P

HEADS = 12
HD = 64
FF = 3072
WS = 14
GRID = 64
WMB = 3
WT = 196
ROWS = 588


def layer_norm(values, gain_vec, shift_vec):
    average = jnp.mean(values, axis=-1, keepdims=True)
    centred = values - average
    spread = jnp.mean(centred * centred, axis=-1, keepdims=True)
    return centred * lax.rsqrt(spread + 1e-06) * gain_vec + shift_vec


def window_mask(slot_ids):
    across = (GRID + WS - 1) // WS
    row_pos = lax.broadcasted_iota(jnp.int32, (WS, WS), 0)
    col_pos = lax.broadcasted_iota(jnp.int32, (WS, WS), 1)
    win_row = (slot_ids // across)[:, None, None]
    win_col = (slot_ids % across)[:, None, None]
    inside = (
        (slot_ids < across * across)[:, None, None]
        & (win_row * WS + row_pos < GRID)
        & (win_col * WS + col_pos < GRID)
    )
    return inside.astype(jnp.float32).reshape(-1)


def offset_picks():
    offsets = (
        lax.broadcasted_iota(jnp.int32, (WS, WS), 0)
        - lax.broadcasted_iota(jnp.int32, (WS, WS), 1)
        + (WS - 1)
    )
    slots_iota = lax.broadcasted_iota(jnp.int32, (WS, WS, 2 * WS - 1), 2)
    return (offsets[:, :, None] == slots_iota).astype(jnp.float32)


def score_block(query_win, key_win, table_height, table_width, head_scale):
    scores = (
        jnp.einsum("wijhc,wklhc->whijkl", query_win, key_win, preferred_element_type=jnp.float32)
        * head_scale
    )
    rel_rows = jnp.einsum(
        "wijhc,ikc->whijk", query_win, table_height, preferred_element_type=jnp.float32
    )
    rel_cols = jnp.einsum(
        "wijhc,jlc->whijl", query_win, table_width, preferred_element_type=jnp.float32
    )
    scores = scores + rel_rows[:, :, :, :, :, None] + rel_cols[:, :, :, :, None, :]
    return scores.reshape(WMB, query_win.shape[3], WT, WT)


def per_device(
    tokens,
    window_ids,
    norm1_gain,
    norm1_bias,
    qkv_weight,
    qv_bias,
    rel_height,
    rel_width,
    proj_weight,
    proj_bias,
    norm2_gain,
    norm2_bias,
    fc1_weight,
    fc1_bias,
    fc2_weight,
    fc2_bias,
    out_grad,
):
    high = lax.Precision.HIGHEST
    head_scale = 1.0 / math.sqrt(HD)
    tensor_rank = lax.axis_index("tensor")
    local_rows = tokens.shape[2]
    model_width = tokens.shape[3]
    block_count = tokens.shape[0] * tokens.shape[1]
    tok_blocks = tokens.reshape(block_count, local_rows, model_width)
    cot_blocks = out_grad.reshape(block_count, local_rows, model_width)
    id_blocks = window_ids.reshape(block_count, window_ids.shape[2])
    head_cols = qkv_weight.shape[2]
    local_heads = head_cols // HD
    hidden_cols = fc1_weight.shape[1]
    gain_one = norm1_gain.astype(jnp.float32)
    shift_one = norm1_bias.astype(jnp.float32)
    gain_two = norm2_gain.astype(jnp.float32)
    shift_two = norm2_bias.astype(jnp.float32)
    proj_shift = proj_bias.astype(jnp.float32)
    fc1_shift = fc1_bias.astype(jnp.float32)
    fc2_shift = fc2_bias.astype(jnp.float32)
    qkv_shift = jnp.stack(
        [
            qv_bias[0].astype(jnp.float32),
            jnp.zeros((head_cols,), jnp.float32),
            qv_bias[1].astype(jnp.float32),
        ]
    )
    picks = offset_picks()
    table_height = jnp.einsum(
        "ikd,dc->ikc", picks.astype(jnp.bfloat16), rel_height, preferred_element_type=jnp.float32
    ).astype(jnp.bfloat16)
    table_width = jnp.einsum(
        "ikd,dc->ikc", picks.astype(jnp.bfloat16), rel_width, preferred_element_type=jnp.float32
    ).astype(jnp.bfloat16)
    height_high = table_height.astype(jnp.float32)
    width_high = table_width.astype(jnp.float32)
    shards = (qkv_weight, proj_weight, fc1_weight, fc2_weight)
    big_init = tuple((jnp.zeros(item.shape, jnp.float32) for item in shards))
    small_init = (
        jnp.zeros((6, model_width), jnp.float32),
        jnp.zeros((2, WS, WS, HD), jnp.float32),
        jnp.zeros((2, head_cols), jnp.float32),
        jnp.zeros((hidden_cols,), jnp.float32),
    )

    def run_block(carry, inputs):
        big_acc, small_acc = carry
        rows_in, ids_block, cot_rows = inputs
        whole = (
            lax.all_gather(shards[0], ("dp", "win"), axis=0, tiled=True),
            lax.all_gather(shards[1], ("dp", "win"), axis=1, tiled=True),
            lax.all_gather(shards[2], ("dp", "win"), axis=0, tiled=True),
            lax.all_gather(shards[3], ("dp", "win"), axis=1, tiled=True),
        )
        qkv_full, proj_full, fc1_full, fc2_full = whole
        mask_all = window_mask(ids_block)
        mask_rows = lax.dynamic_slice_in_dim(mask_all, tensor_rank * local_rows, local_rows)[
            :, None
        ]
        rows_high = rows_in.astype(jnp.float32)

        def first_norm(values, gain_vec, shift_vec):
            return mask_rows * layer_norm(values, gain_vec, shift_vec)

        normed = first_norm(rows_high, gain_one, shift_one).astype(jnp.bfloat16)
        normed_all = lax.all_gather(normed, "tensor", axis=0, tiled=True)
        projected = jnp.einsum(
            "rd,dtc->rtc", normed_all, qkv_full, preferred_element_type=jnp.float32
        )
        projected = (projected + qkv_shift).astype(jnp.bfloat16)
        shape_five = (WMB, WS, WS, local_heads, HD)
        query_win = projected[:, 0, :].reshape(shape_five)
        key_win = projected[:, 1, :].reshape(shape_five)
        value_win = projected[:, 2, :].reshape(WMB, WT, local_heads, HD)
        scores = score_block(query_win, key_win, table_height, table_width, head_scale)
        top_score = jnp.max(scores, axis=-1, keepdims=True)
        log_total = top_score + jnp.log(
            jnp.sum(jnp.exp(scores - top_score), axis=-1, keepdims=True)
        )
        probs_low = jnp.exp(scores - log_total).astype(jnp.bfloat16)
        attended = jnp.einsum(
            "whqk,wkhc->wqhc", probs_low, value_win, preferred_element_type=jnp.float32
        )
        attended = attended.reshape(ROWS, head_cols).astype(jnp.bfloat16)
        branch = lax.psum_scatter(
            jnp.dot(attended, proj_full, preferred_element_type=jnp.float32),
            "tensor",
            scatter_dimension=0,
            tiled=True,
        )
        hidden = rows_high + mask_rows * (branch + proj_shift)
        normed2 = layer_norm(hidden, gain_two, shift_two).astype(jnp.bfloat16)
        normed2_all = lax.all_gather(normed2, "tensor", axis=0, tiled=True)
        upper = jnp.dot(normed2_all, fc1_full, preferred_element_type=jnp.float32) + fc1_shift
        activ = jax.nn.gelu(upper, approximate=False).astype(jnp.bfloat16)
        mixed = (
            lax.psum_scatter(
                jnp.dot(activ, fc2_full, preferred_element_type=jnp.float32).astype(jnp.bfloat16),
                "tensor",
                scatter_dimension=0,
                tiled=True,
            ).astype(jnp.float32)
            + fc2_shift
        )
        result = (mask_rows * (hidden + mixed)).astype(jnp.bfloat16)
        grad_mixed = mask_rows * cot_rows.astype(jnp.float32)
        grad_fc2_shift = jnp.sum(grad_mixed, axis=0)
        grad_mixed_all = lax.all_gather(
            grad_mixed.astype(jnp.bfloat16), "tensor", axis=0, tiled=True
        )
        grad_fc2_full = jnp.einsum(
            "rf,rd->fd", activ, grad_mixed_all, preferred_element_type=jnp.float32
        )
        grad_activ = jnp.einsum(
            "rd,fd->rf", grad_mixed_all, fc2_full, preferred_element_type=jnp.float32
        )
        _, gelu_back = jax.vjp(partial(jax.nn.gelu, approximate=False), upper)
        grad_upper = gelu_back(grad_activ)[0].astype(jnp.bfloat16)
        grad_fc1_shift = jnp.sum(grad_upper, axis=0, dtype=jnp.float32)
        grad_fc1_full = jnp.einsum(
            "rd,rf->df", normed2_all, grad_upper, preferred_element_type=jnp.float32
        )
        grad_normed2 = lax.psum_scatter(
            jnp.einsum("rf,df->rd", grad_upper, fc1_full, preferred_element_type=jnp.float32),
            "tensor",
            scatter_dimension=0,
            tiled=True,
        )
        _, second_back = jax.vjp(layer_norm, hidden, gain_two, shift_two)
        grad_hid_norm, grad_gain_two, grad_shift_two = second_back(grad_normed2)
        grad_hidden = grad_mixed + grad_hid_norm
        grad_branch = mask_rows * grad_hidden
        grad_proj_shift = jnp.sum(grad_branch, axis=0)
        grad_branch_all = lax.all_gather(
            grad_branch.astype(jnp.bfloat16), "tensor", axis=0, tiled=True
        )
        grad_proj_full = jnp.einsum(
            "rc,rd->cd", attended, grad_branch_all, preferred_element_type=jnp.float32
        )
        grad_attended = jnp.einsum(
            "rd,cd->rc", grad_branch_all, proj_full, preferred_element_type=jnp.float32
        ).astype(jnp.bfloat16)
        again = score_block(query_win, key_win, table_height, table_width, head_scale)
        probs = jnp.exp(again - log_total)
        probs_again = probs.astype(jnp.bfloat16)
        grad_att_win = grad_attended.reshape(WMB, WT, local_heads, HD)
        grad_probs = jnp.einsum(
            "wqhc,wkhc->whqk", grad_att_win, value_win, preferred_element_type=jnp.float32
        )
        grad_values = jnp.einsum(
            "whqk,wqhc->wkhc", probs_again, grad_att_win, preferred_element_type=jnp.float32
        )
        grad_values = grad_values.reshape(ROWS, head_cols).astype(jnp.bfloat16)
        inner_sum = jnp.sum(probs * grad_probs, axis=-1, keepdims=True)
        grad_scores = (probs * (grad_probs - inner_sum)).astype(jnp.bfloat16)
        grad_six = grad_scores.reshape(WMB, local_heads, WS, WS, WS, WS)
        grad_high = grad_six.astype(jnp.float32)
        row_sums = jnp.sum(grad_high, axis=5)
        col_sums = jnp.sum(grad_high, axis=4)
        grad_query = (
            jnp.einsum("whijkl,wklhc->wijhc", grad_six, key_win, preferred_element_type=jnp.float32)
            * head_scale
        )
        grad_query = grad_query + jnp.einsum(
            "whijk,ikc->wijhc", row_sums, height_high, precision=high
        )
        grad_query = grad_query + jnp.einsum(
            "whijl,jlc->wijhc", col_sums, width_high, precision=high
        )
        grad_keys = (
            jnp.einsum(
                "whijkl,wijhc->wklhc", grad_six, query_win, preferred_element_type=jnp.float32
            )
            * head_scale
        )
        query_high = query_win.astype(jnp.float32)
        grad_table_height = jnp.einsum("whijk,wijhc->ikc", row_sums, query_high, precision=high)
        grad_table_width = jnp.einsum("whijl,wijhc->jlc", col_sums, query_high, precision=high)
        grad_qkv_rows = jnp.stack(
            [
                grad_query.reshape(ROWS, head_cols).astype(jnp.bfloat16),
                grad_keys.reshape(ROWS, head_cols).astype(jnp.bfloat16),
                grad_values,
            ],
            axis=1,
        )
        grad_qv_shift = jnp.stack(
            [
                jnp.sum(grad_qkv_rows[:, 0, :], axis=0, dtype=jnp.float32),
                jnp.sum(grad_values, axis=0, dtype=jnp.float32),
            ]
        )
        grad_qkv_full = jnp.einsum(
            "rd,rtc->dtc", normed_all, grad_qkv_rows, preferred_element_type=jnp.float32
        )
        grad_normed = lax.psum_scatter(
            jnp.einsum(
                "rtc,dtc->rd", grad_qkv_rows, qkv_full, preferred_element_type=jnp.float32
            ).astype(jnp.bfloat16),
            "tensor",
            scatter_dimension=0,
            tiled=True,
        ).astype(jnp.float32)
        _, first_back = jax.vjp(first_norm, rows_high, gain_one, shift_one)
        grad_in_norm, grad_gain_one, grad_shift_one = first_back(grad_normed)
        grad_rows = grad_hidden + grad_in_norm
        local_big = (grad_qkv_full, grad_proj_full, grad_fc1_full, grad_fc2_full)
        summed = (
            lax.psum_scatter(local_big[0], ("dp", "win"), scatter_dimension=0, tiled=True),
            lax.psum_scatter(local_big[1], ("dp", "win"), scatter_dimension=1, tiled=True),
            lax.psum_scatter(local_big[2], ("dp", "win"), scatter_dimension=0, tiled=True),
            lax.psum_scatter(local_big[3], ("dp", "win"), scatter_dimension=1, tiled=True),
        )
        big_acc = tuple((acc_val + new_val for acc_val, new_val in zip(big_acc, summed)))
        small_new = (
            jnp.stack(
                [
                    grad_gain_one,
                    grad_shift_one,
                    grad_proj_shift,
                    grad_gain_two,
                    grad_shift_two,
                    grad_fc2_shift,
                ]
            ),
            jnp.stack([grad_table_height, grad_table_width]),
            grad_qv_shift,
            grad_fc1_shift,
        )
        small_acc = tuple((acc_val + new_val for acc_val, new_val in zip(small_acc, small_new)))
        return ((big_acc, small_acc), (result, grad_rows))

    (big_acc, small_acc), (outputs, grads_in) = lax.scan(
        run_block, (big_init, small_init), (tok_blocks, id_blocks, cot_blocks)
    )
    vector_sums, table_sums, qv_local, fc1_local = small_acc
    table_grads = jnp.einsum("ikd,sikc->sdc", picks, table_sums, precision=high)
    qv_padded = lax.dynamic_update_slice(
        jnp.zeros((2, HEADS * HD), jnp.float32), qv_local, (0, tensor_rank * head_cols)
    )
    fc1_padded = lax.dynamic_update_slice(
        jnp.zeros((FF,), jnp.float32), fc1_local, (tensor_rank * hidden_cols,)
    )
    vector_sums, table_grads, qv_padded, fc1_padded = lax.psum(
        (vector_sums, table_grads, qv_padded, fc1_padded), ("dp", "win", "tensor")
    )
    output = outputs.reshape(tokens.shape)
    grad_tokens = grads_in.reshape(tokens.shape)
    return (
        output,
        grad_tokens,
        vector_sums[0],
        vector_sums[1],
        big_acc[0],
        qv_padded,
        table_grads[0],
        table_grads[1],
        big_acc[1],
        vector_sums[2],
        vector_sums[3],
        vector_sums[4],
        big_acc[2],
        fc1_padded,
        big_acc[3],
        vector_sums[5],
    )


def solution(mesh):
    in_specs = (
        P("dp", "win", "tensor", None),
        P("dp", "win", None),
        P(),
        P(),
        P(("dp", "win"), None, "tensor"),
        P(None, "tensor"),
        P(),
        P(),
        P("tensor", ("dp", "win")),
        P(),
        P(),
        P(),
        P(("dp", "win"), "tensor"),
        P("tensor"),
        P("tensor", ("dp", "win")),
        P(),
        P("dp", "win", "tensor", None),
    )
    out_specs = (
        P("dp", "win", "tensor", None),
        P("dp", "win", "tensor", None),
        P(),
        P(),
        P(("dp", "win"), None, "tensor"),
        P(),
        P(),
        P(),
        P("tensor", ("dp", "win")),
        P(),
        P(),
        P(),
        P(("dp", "win"), "tensor"),
        P(),
        P("tensor", ("dp", "win")),
        P(),
    )
    return jax.shard_map(
        per_device, mesh=mesh, in_specs=in_specs, out_specs=out_specs, check_vma=False
    )
```

profile of v0, /device:TPU:0, one launch (start us, length us, event | category | flops | bytes accessed | tf_op | source)
XLA Modules:
  0.0 1541.5 jit_solution(1485226767118144920)
XLA Ops:
  22.3 1463.5 %while.31 = (s32[]{:T(128)}, f32[96,3,192]{2,0,1:T(8,128)}, f32[192,96]{1,0:T(8,128)}, f32[96,768]{1,0:T(8,128)}, f32[768,96]{0,1:T(8,128)}, /*index=5*/f32[6,76...) while((s32[]{:T(128)}, f32[96,3,192]{2,0,1:T(8,128)}, ...), condition=%wide.region_31.32_spmd.clone, body=%wide.region_0.31_spmd.clone.sunk | while | flops 6651830272 | bytes 234217168 | solution.py:315
  26.8 22.9 %all-gather.12 = bf16[4,147,768]{2,1,0:T(8,128)(2,1)S(1)} all-gather(bf16[1,147,768]{2,1,0:T(8,128)(2,1)S(1)} %fusion.268), channel_id=1, replica_groups=mesh['dp'=2,'win'=4,'tensor'=4] {'tensor'}, dimensions={0}, use_global_device_ids=true | all-gather | bytes 1128960 | tf_op jit(solution)/shard_map/while/body/eval_jaxpr/all_gather | solution.py:148
  132.4 39.6 %fusion.274 = f32[152,768]{1,0:T(8,128)} fusion(f32[588,768]{1,0:T(8,128)} %fusion.273), kind=kCustom, calls=%all-reduce-scatter.clone.1 | all-reduce-scatter fusion | flops 466945 | bytes 2273792 | tf_op jit(solution)/shard_map/while
  181.0 20.2 %all-gather.13 = bf16[4,147,768]{2,1,0:T(8,128)(2,1)} all-gather(bf16[1,147,768]{2,1,0:T(8,128)(2,1)S(1)} %fusion.277), channel_id=1, replica_groups=mesh['dp'=2,'win'=4,'tensor'=4] {'tensor'}, dimensions={0}, use_global_device_ids=true | all-gather | bytes 1128960 | tf_op jit(solution)/shard_map/while/body/eval_jaxpr/all_gather | solution.py:175
  203.7 19.1 %all-gather.14 = bf16[4,147,768]{2,1,0:T(8,128)(2,1)} all-gather(bf16[1,147,768]{2,1,0:T(8,128)(2,1)S(1)} %copy-done.22), channel_id=1, replica_groups=mesh['dp'=2,'win'=4,'tensor'=4] {'tensor'}, dimensions={0}, use_global_device_ids=true | all-gather | bytes 1128960 | tf_op jit(solution)/shard_map/while/body/eval_jaxpr/all_gather | solution.py:190
  240.4 32.7 %fusion.280 = f32[152,768]{1,0:T(8,128)S(1)} fusion(f32[588,768]{1,0:T(8,128)} %fusion.279), kind=kCustom, calls=%all-reduce-scatter.1.clone.1 | all-reduce-scatter fusion | flops 466945 | bytes 2273792 | tf_op jit(solution)/shard_map/while
  382.2 27.7 %fusion.290 = (bf16[152,768]{1,0:T(8,128)(2,1)S(1)}, bf16[152,768]{1,0:T(8,128)(2,1)S(1)}) fusion(bf16[588,768]{1,0:T(8,128)(2,1)} %bitcast_convert_fusion.2, bf16[588,768]{1,0:T(8,128)(2,1)} %convolution_convert_fusion.9), kind=kCustom, calls=%all-reduce-scatter.4.clone.1 | all-reduce-scatter fusion | flops 933889 | bytes 2273792 | tf_op jit(solution)/shard_map/while
  428.3 37.0 %reduce-scatter.23.cloned.1.call-done = f32[768,96]{0,1:T(8,128)} async-done(((f32[768,768]{0,1:T(8,128)}), f32[768,96]{0,1:T(8,128)}) %reduce-scatter.23.cloned.1.call-update) | async-done | bytes 294928 | tf_op jit(solution)/shard_map/while/body/eval_jaxpr/reduce_scatter | solution.py:294
  466.3 44.5 %reduce-scatter.21.cloned.1.call-done = f32[96,768]{1,0:T(8,128)} async-done(((f32[768,768]{1,0:T(8,128)}), f32[96,768]{1,0:T(8,128)}) %reduce-scatter.21.cloned.1.call-update) | async-done | bytes 294928 | tf_op jit(solution)/shard_map/while/body/eval_jaxpr/reduce_scatter | solution.py:293
  517.3 21.2 %all-gather.12 = bf16[4,147,768]{2,1,0:T(8,128)(2,1)S(1)} all-gather(bf16[1,147,768]{2,1,0:T(8,128)(2,1)S(1)} %fusion.268), channel_id=1, replica_groups=mesh['dp'=2,'win'=4,'tensor'=4] {'tensor'}, dimensions={0}, use_global_device_ids=true | all-gather | bytes 1128960 | tf_op jit(solution)/shard_map/while/body/eval_jaxpr/all_gather | solution.py:148
  620.3 39.6 %fusion.274 = f32[152,768]{1,0:T(8,128)} fusion(f32[588,768]{1,0:T(8,128)} %fusion.273), kind=kCustom, calls=%all-reduce-scatter.clone.1 | all-reduce-scatter fusion | flops 466945 | bytes 2273792 | tf_op jit(solution)/shard_map/while
  668.8 20.4 %all-gather.13 = bf16[4,147,768]{2,1,0:T(8,128)(2,1)} all-gather(bf16[1,147,768]{2,1,0:T(8,128)(2,1)S(1)} %fusion.277), channel_id=1, replica_groups=mesh['dp'=2,'win'=4,'tensor'=4] {'tensor'}, dimensions={0}, use_global_device_ids=true | all-gather | bytes 1128960 | tf_op jit(solution)/shard_map/while/body/eval_jaxpr/all_gather | solution.py:175
  728.3 31.4 %fusion.280 = f32[152,768]{1,0:T(8,128)S(1)} fusion(f32[588,768]{1,0:T(8,128)} %fusion.279), kind=kCustom, calls=%all-reduce-scatter.1.clone.1 | all-reduce-scatter fusion | flops 466945 | bytes 2273792 | tf_op jit(solution)/shard_map/while
  867.9 26.9 %fusion.290 = (bf16[152,768]{1,0:T(8,128)(2,1)S(1)}, bf16[152,768]{1,0:T(8,128)(2,1)S(1)}) fusion(bf16[588,768]{1,0:T(8,128)(2,1)} %bitcast_convert_fusion.2, bf16[588,768]{1,0:T(8,128)(2,1)} %convolution_convert_fusion.9), kind=kCustom, calls=%all-reduce-scatter.4.clone.1 | all-reduce-scatter fusion | flops 933889 | bytes 2273792 | tf_op jit(solution)/shard_map/while
  913.6 36.9 %reduce-scatter.23.cloned.1.call-done = f32[768,96]{0,1:T(8,128)} async-done(((f32[768,768]{0,1:T(8,128)}), f32[768,96]{0,1:T(8,128)}) %reduce-scatter.23.cloned.1.call-update) | async-done | bytes 294928 | tf_op jit(solution)/shard_map/while/body/eval_jaxpr/reduce_scatter | solution.py:294
  951.6 44.5 %reduce-scatter.21.cloned.1.call-done = f32[96,768]{1,0:T(8,128)} async-done(((f32[768,768]{1,0:T(8,128)}), f32[96,768]{1,0:T(8,128)}) %reduce-scatter.21.cloned.1.call-update) | async-done | bytes 294928 | tf_op jit(solution)/shard_map/while/body/eval_jaxpr/reduce_scatter | solution.py:293
  1002.6 21.2 %all-gather.12 = bf16[4,147,768]{2,1,0:T(8,128)(2,1)S(1)} all-gather(bf16[1,147,768]{2,1,0:T(8,128)(2,1)S(1)} %fusion.268), channel_id=1, replica_groups=mesh['dp'=2,'win'=4,'tensor'=4] {'tensor'}, dimensions={0}, use_global_device_ids=true | all-gather | bytes 1128960 | tf_op jit(solution)/shard_map/while/body/eval_jaxpr/all_gather | solution.py:148
  1105.6 39.6 %fusion.274 = f32[152,768]{1,0:T(8,128)} fusion(f32[588,768]{1,0:T(8,128)} %fusion.273), kind=kCustom, calls=%all-reduce-scatter.clone.1 | all-reduce-scatter fusion | flops 466945 | bytes 2273792 | tf_op jit(solution)/shard_map/while
  1154.1 20.4 %all-gather.13 = bf16[4,147,768]{2,1,0:T(8,128)(2,1)} all-gather(bf16[1,147,768]{2,1,0:T(8,128)(2,1)S(1)} %fusion.277), channel_id=1, replica_groups=mesh['dp'=2,'win'=4,'tensor'=4] {'tensor'}, dimensions={0}, use_global_device_ids=true | all-gather | bytes 1128960 | tf_op jit(solution)/shard_map/while/body/eval_jaxpr/all_gather | solution.py:175
  1213.6 31.4 %fusion.280 = f32[152,768]{1,0:T(8,128)S(1)} fusion(f32[588,768]{1,0:T(8,128)} %fusion.279), kind=kCustom, calls=%all-reduce-scatter.1.clone.1 | all-reduce-scatter fusion | flops 466945 | bytes 2273792 | tf_op jit(solution)/shard_map/while
  1353.4 25.8 %fusion.290 = (bf16[152,768]{1,0:T(8,128)(2,1)S(1)}, bf16[152,768]{1,0:T(8,128)(2,1)S(1)}) fusion(bf16[588,768]{1,0:T(8,128)(2,1)} %bitcast_convert_fusion.2, bf16[588,768]{1,0:T(8,128)(2,1)} %convolution_convert_fusion.9), kind=kCustom, calls=%all-reduce-scatter.4.clone.1 | all-reduce-scatter fusion | flops 933889 | bytes 2273792 | tf_op jit(solution)/shard_map/while
  1397.9 37.8 %reduce-scatter.23.cloned.1.call-done = f32[768,96]{0,1:T(8,128)} async-done(((f32[768,768]{0,1:T(8,128)}), f32[768,96]{0,1:T(8,128)}) %reduce-scatter.23.cloned.1.call-update) | async-done | bytes 294928 | tf_op jit(solution)/shard_map/while/body/eval_jaxpr/reduce_scatter | solution.py:294
  1436.8 44.5 %reduce-scatter.21.cloned.1.call-done = f32[96,768]{1,0:T(8,128)} async-done(((f32[768,768]{1,0:T(8,128)}), f32[96,768]{1,0:T(8,128)}) %reduce-scatter.21.cloned.1.call-update) | async-done | bytes 294928 | tf_op jit(solution)/shard_map/while/body/eval_jaxpr/reduce_scatter | solution.py:293
  1488.8 41.0 %all-reduce.8 = (f32[6,768]{1,0:T(8,128)S(1)}, f32[2,768]{1,0:T(2,128)}, f32[2,27,64]{2,1,0:T(8,128)S(1)}, f32[3072]{0:T(1024)}) all-reduce(f32[6,768]{1,0:T(8,128)} %get-tuple-element.412, f32[2,768]{1,0:T(2,128)S(1)} %dynamic_update_slice.20, ...), channel_id=1, replica_groups=mesh['dp'=2,'win'=4,'tensor'=4] {'dp','win','tensor'}, use_global_device_ids=true, to_apply=%region_32.33 | all-reduce | flops 12672 | bytes 101376 | tf_op jit(solution)/shard_map/psum | solution.py:326
  (831 shorter events, 793.0 us)
Async XLA Ops:
  22.3 202.7 %all-gather.19.cloned.1.call-start = ((), (), s32[]{:S(2)}) async-start(), calls=%async_computation.4 | async-start | bytes 1327104 | tf_op jit(solution)/shard_map/while/body/eval_jaxpr/all_gather | solution.py:134
  23.1 205.8 %all-gather.21.cloned.1.call-start = ((), (), s32[]{:S(2)}) async-start(), calls=%async_computation.5 | async-start | bytes 1327104 | tf_op jit(solution)/shard_map/while/body/eval_jaxpr/all_gather | solution.py:135
  175.0 250.5 %reduce-scatter.19.cloned.1.call-start = ((), (), s32[]{:S(2)}) async-start(), calls=%async_computation.7 | async-start | bytes 884736 | tf_op jit(solution)/shard_map/while
  339.7 86.8 %reduce-scatter.17.cloned.1.call-start = ((), (), s32[]{:S(2)}) async-start(), calls=%async_computation.6 | async-start | bytes 2654208 | tf_op jit(solution)/shard_map/while/body/eval_jaxpr/reduce_scatter | solution.py:291
  362.8 102.4 %reduce-scatter.23.cloned.1.call-start = ((), (), s32[]{:S(2)}) async-start(), calls=%async_computation.9 | async-start | bytes 2654208 | tf_op jit(solution)/shard_map/while/body/eval_jaxpr/reduce_scatter | solution.py:294
  369.7 141.1 %reduce-scatter.21.cloned.1.call-start = ((), (), s32[]{:S(2)}) async-start(), calls=%async_computation.8 | async-start | bytes 2654208 | tf_op jit(solution)/shard_map/while/body/eval_jaxpr/reduce_scatter | solution.py:293
  409.9 10.1 collective-permute-start.2
  412.9 10.1 collective-permute-start.3
  512.8 200.2 %all-gather.19.cloned.1.call-start = ((), (), s32[]{:S(2)}) async-start(), calls=%async_computation.4 | async-start | bytes 1327104 | tf_op jit(solution)/shard_map/while/body/eval_jaxpr/all_gather | solution.py:134
  513.5 203.2 %all-gather.21.cloned.1.call-start = ((), (), s32[]{:S(2)}) async-start(), calls=%async_computation.5 | async-start | bytes 1327104 | tf_op jit(solution)/shard_map/while/body/eval_jaxpr/all_gather | solution.py:135
  662.7 248.0 %reduce-scatter.19.cloned.1.call-start = ((), (), s32[]{:S(2)}) async-start(), calls=%async_computation.7 | async-start | bytes 884736 | tf_op jit(solution)/shard_map/while
  825.5 86.3 %reduce-scatter.17.cloned.1.call-start = ((), (), s32[]{:S(2)}) async-start(), calls=%async_computation.6 | async-start | bytes 2654208 | tf_op jit(solution)/shard_map/while/body/eval_jaxpr/reduce_scatter | solution.py:291
  848.6 102.0 %reduce-scatter.23.cloned.1.call-start = ((), (), s32[]{:S(2)}) async-start(), calls=%async_computation.9 | async-start | bytes 2654208 | tf_op jit(solution)/shard_map/while/body/eval_jaxpr/reduce_scatter | solution.py:294
  855.4 140.7 %reduce-scatter.21.cloned.1.call-start = ((), (), s32[]{:S(2)}) async-start(), calls=%async_computation.8 | async-start | bytes 2654208 | tf_op jit(solution)/shard_map/while/body/eval_jaxpr/reduce_scatter | solution.py:293
  894.9 10.4 collective-permute-start.2
  897.8 10.5 collective-permute-start.3
  998.1 200.2 %all-gather.19.cloned.1.call-start = ((), (), s32[]{:S(2)}) async-start(), calls=%async_computation.4 | async-start | bytes 1327104 | tf_op jit(solution)/shard_map/while/body/eval_jaxpr/all_gather | solution.py:134
  998.8 203.2 %all-gather.21.cloned.1.call-start = ((), (), s32[]{:S(2)}) async-start(), calls=%async_computation.5 | async-start | bytes 1327104 | tf_op jit(solution)/shard_map/while/body/eval_jaxpr/all_gather | solution.py:135
  1148.0 247.0 %reduce-scatter.19.cloned.1.call-start = ((), (), s32[]{:S(2)}) async-start(), calls=%async_computation.7 | async-start | bytes 884736 | tf_op jit(solution)/shard_map/while
  1310.9 85.1 %reduce-scatter.17.cloned.1.call-start = ((), (), s32[]{:S(2)}) async-start(), calls=%async_computation.6 | async-start | bytes 2654208 | tf_op jit(solution)/shard_map/while/body/eval_jaxpr/reduce_scatter | solution.py:291
  1334.0 101.8 %reduce-scatter.23.cloned.1.call-start = ((), (), s32[]{:S(2)}) async-start(), calls=%async_computation.9 | async-start | bytes 2654208 | tf_op jit(solution)/shard_map/while/body/eval_jaxpr/reduce_scatter | solution.py:294
  1340.9 140.5 %reduce-scatter.21.cloned.1.call-start = ((), (), s32[]{:S(2)}) async-start(), calls=%async_computation.8 | async-start | bytes 2654208 | tf_op jit(solution)/shard_map/while/body/eval_jaxpr/reduce_scatter | solution.py:293
  1379.2 10.3 collective-permute-start.2
  1382.0 10.5 collective-permute-start.3
  (192 other events, 2769.5 us)
Sparse Core Ops, SparseCore 0:
  25.0 26.6 all-gather.18
  175.1 21.1 all-gather.20
  339.9 34.2 reduce-scatter.18
  377.3 42.3 reduce-scatter.16
  422.9 42.3 reduce-scatter.22
  468.4 42.3 reduce-scatter.20
  515.5 23.9 all-gather.18
  662.8 21.1 all-gather.20
  825.6 33.5 reduce-scatter.18
  862.4 42.3 reduce-scatter.16
  908.2 42.3 reduce-scatter.22
  953.7 42.3 reduce-scatter.20
  1000.8 23.9 all-gather.18
  1148.1 21.1 all-gather.20
  1311.0 33.5 reduce-scatter.18
  1347.8 42.3 reduce-scatter.16
  1393.4 42.3 reduce-scatter.22
  1438.9 42.3 reduce-scatter.20
where the time goes:
time: 1550 us; the launch traced here: 1540 us
  blocking collectives  635 us (41%)
  local copies, waits for them, and re-layouts  292 us (19%)
  waiting for transfers between devices  249 us (16%)
  matrix products  205 us (13%)
  other arithmetic  107 us (7%)
  starting transfers between devices  31.2 us (2%)
    while x9, blocking collectives  295 us
    reduce_scatter x3, waiting for transfers between devices, run_block(): lax.psum_scatter(local_big[2], ('dp', 'win'), scatter_dimension=0, tiled=...  134 us
    reduce_scatter x3, waiting for transfers between devices, run_block(): lax.psum_scatter(local_big[3], ('dp', 'win'), scatter_dimension=1, tiled=...  112 us
    reshape x6, local copies, waits for them, and re-layouts, score_block(): return scores.reshape(WMB, query_win.shape[3], WT, WT)  80.6 us
    while x411, local copies, waits for them, and re-layouts  79.5 us
    all_gather x3, blocking collectives, run_block(): normed_all = lax.all_gather(normed, 'tensor', axis=0, tiled=True)  65.3 us
    all_gather x3, blocking collectives, run_block(): normed2_all = lax.all_gather(normed2, 'tensor', axis=0, tiled=True)  61.1 us
    all_gather x3, blocking collectives, run_block(): lax.all_gather(grad_mixed.astype(jnp.bfloat16), 'tensor', axis=0, tiled=T...  57.1 us
  transfers between devices with their start and end apart: 30, of which 9 were waited for; matrix products, arithmetic and copies ran while one was open for 38% of the time, Pallas kernels for 0%

commit v1 on v0

v1 whole, which is shorter than its diff:
```python
import math
from functools import partial

import jax
import jax.numpy as jnp
import numpy as np
from jax import lax
from jax.experimental import pallas as pl
from jax.experimental.pallas import tpu as pltpu
from jax.sharding import PartitionSpec as P

HEADS = 12
HD = 64
WS = 14
GRID = 64
WT = 196
BT = 49
BP = 56
WR = 4 * BP
QR = 64
NR = 2 * WR + QR
NE = NR + WR
BF = jnp.bfloat16
F32 = jnp.float32

WINDOWS_OF = (((0, 0), (1, 0)), ((2, 0), (0, 1)), ((2, 2), (2, 1)), ((0, 2), (1, 2)))
SHARED = (1, 1)


def block_table():
    rows = []
    for dev in range(4):
        row = []
        for m, s in WINDOWS_OF[dev]:
            row += [m * 12 + 4 * s + j for j in range(4)]
        row.append(SHARED[0] * 12 + 4 * SHARED[1] + dev)
        row += [SHARED[0] * 12 + 4 * SHARED[1] + j for j in range(4)]
        rows.append(row)
    return np.array(rows, np.int32)


def home_table():
    table = block_table()
    place = {}
    for dev in range(4):
        for slot in range(9):
            place[int(table[dev, slot])] = dev * 9 + slot
    return np.array([[place[m * 12 + 3 * dev + b] for m in range(3) for b in range(3)] for dev in range(4)], np.int32)


def token_positions():
    row = np.arange(WR)
    off = row % BP
    token = (row // BP) * BT + np.minimum(off, BT - 1)
    return token // WS, token % WS, off < BT


def key_tail():
    i, j, valid = token_positions()
    tail = np.zeros((WR, 128), np.float32)
    for m in range(WS):
        tail[:, 64 + m] = i == m
        tail[:, 78 + m] = j == m
    tail[:, 92:120] = tail[:, 64:92]
    tail[:, :120] *= valid[:, None]
    tail[:, 120] = np.where(valid, 0.0, -1e30)
    return tail


def pick_lanes(i, j):
    lane = np.arange(128)[None, :]
    m = np.clip((lane - 64) % 28, 0, 27)
    is_w = m >= 14
    fwd = jnp.where(is_w, 32 + j[:, None] - (m - 14) + 13, i[:, None] - m + 13)
    fwd = jnp.where((lane >= 64) & (lane < 120), fwd, 0)
    d = lane % 32
    pos = jnp.where(lane >= 32, j[:, None], i[:, None]) + 13 - d
    ok = (pos >= 0) & (pos < WS) & (lane < 64) & (d < 27)
    back = jnp.where(ok, pos + jnp.where(lane >= 32, 78, 64), 127)
    return fwd.astype(jnp.int32), back.astype(jnp.int32)


def dotf(a, b, dims):
    return lax.dot_general(a, b, (dims, ((), ())), preferred_element_type=F32)


NN = ((1,), (0,))
NT = ((1,), (1,))
TN = ((0,), (0,))


def compute_kernel(
    x_ref, cot_ref, mask_ref, w_ref, vec_ref, qkvb_ref, fc1b_ref, ktail_ref, fwd_ref, back_ref, tab_ref, tabt_ref,
    out_ref, gn_ref, gh_ref, g_ref, vg_ref, tg_ref,
    nrm, proj, qaug, kaug, vals, probs, att, hid, nr2, mix, gn2, act, gup, gml, gbl, dqkv,
):
    g1, b1, pb, g2, b2, fb = (vec_ref[i : i + 1, :] for i in range(6))

    def stats(v):
        mu = jnp.mean(v, axis=-1, keepdims=True)
        c = v - mu
        var = jnp.mean(c * c, axis=-1, keepdims=True)
        return c, lax.rsqrt(var + 1e-6)

    vg_ref[...] = jnp.zeros_like(vg_ref)

    for r0 in range(0, NE, 32):
        rows = slice(r0, r0 + 32)
        c, rs = stats(x_ref[r0 // 8 : r0 // 8 + 4].astype(F32).reshape(32, 768))
        nrm[rows, :] = (mask_ref[rows, :] * (c * rs * g1 + b1)).astype(BF)

    def fwd_t(t, _):
        proj[...] = dotf(nrm[...], w_ref[0, t][:, :576], NN) + qkvb_ref[t]
        for h in range(3):
            hh = 3 * t + h
            qs = (proj[:NR, 64 * h : 64 * h + 64].astype(BF) * BF(0.125)).astype(BF)
            rel = dotf(qs, tabt_ref[...], NN)
            lane = lax.broadcasted_iota(jnp.int32, (NR, 128), 1)
            got = jnp.take_along_axis(rel, fwd_ref[...], axis=1, mode="promise_in_bounds")
            hi = got.astype(BF).astype(F32)
            tail = jnp.where(lane < 92, hi, got - hi)
            tail = jnp.where(lane == 120, 1.0, jnp.where(lane < 120, tail, 0.0)).astype(BF)
            qa = jnp.concatenate([qs, tail[:, 64:]], axis=1)
            qaug[hh] = qa
            for w in range(3):
                src = slice(w * WR, w * WR + WR) if w < 2 else slice(NR, NE)
                k = proj[src, 192 + 64 * h : 256 + 64 * h].astype(BF)
                kaug[hh, w] = jnp.concatenate([k, ktail_ref[:, 64:]], axis=1)
                vals[hh, w] = proj[src, 384 + 64 * h : 448 + 64 * h].astype(BF)
        return 0

    lax.fori_loop(0, 4, fwd_t, 0)
    mix[...] = jnp.zeros_like(mix)

    def att_t(t, _):
        for h in range(3):
            hh = 3 * t + h
            for w in range(3):
                rows = slice(w * WR, w * WR + WR) if w < 2 else slice(2 * WR, NR)
                s = dotf(qaug[hh, rows, :], kaug[hh, w], NT)
                e = jnp.exp(s - jnp.max(s, axis=-1, keepdims=True))
                p = (e * (1.0 / jnp.sum(e, axis=-1, keepdims=True))).astype(BF)
                probs[hh, rows, :] = p
                att[t, rows, 64 * h : 64 * h + 64] = dotf(p, vals[hh, w], NN).astype(BF)
        mix[...] += dotf(att[t], w_ref[0, t][:, 576:], NT)
        return 0

    lax.fori_loop(0, 4, att_t, 0)

    for r0 in range(0, NR, 32):
        rows = slice(r0, r0 + 32)
        x = x_ref[r0 // 8 : r0 // 8 + 4].astype(F32).reshape(32, 768)
        hv = x + mask_ref[rows, :] * (mix[rows, :] + pb)
        hid[rows, :] = hv
        c, rs = stats(hv)
        nr2[rows, :] = (c * rs * g2 + b2).astype(BF)
        gm = mask_ref[rows, :] * cot_ref[r0 // 8 : r0 // 8 + 4].astype(F32).reshape(32, 768)
        gml[rows, :] = gm.astype(BF)
    mix[...] = jnp.zeros_like(mix)
    gn2[...] = jnp.zeros_like(gn2)

    def mlp_t(t, _):
        for f in range(3):
            cols = slice(256 * f, 256 * f + 256)
            for r0 in range(0, NR, 128):
                rows = slice(r0, r0 + 128)
                up = dotf(nr2[rows, :], w_ref[1, t][:, cols], NN) + fc1b_ref[t][:, cols]
                ga = dotf(gml[rows, :], w_ref[2, t][:, cols], NN)
                cdf = 0.5 * (1.0 + lax.erf(up * (1.0 / math.sqrt(2.0))))
                pdf = jnp.exp(-0.5 * up * up) * (1.0 / math.sqrt(2.0 * math.pi))
                act[rows, cols] = (up * cdf).astype(BF)
                gup[rows, cols] = (ga * (cdf + up * pdf)).astype(BF)
        vg_ref[pl.ds(8 + t, 1), :] = jnp.sum(gup[...].astype(F32), axis=0, keepdims=True)
        mix[...] += dotf(act[...], w_ref[2, t], NT)
        gn2[...] += dotf(gup[...], w_ref[1, t], NT)
        g_ref[2, t] = dotf(gml[...], act[...], TN).astype(BF)
        g_ref[1, t] = dotf(nr2[...], gup[...], TN).astype(BF)
        return 0

    lax.fori_loop(0, 4, mlp_t, 0)

    sums = [jnp.zeros((8, 768), F32) for _ in range(4)]

    def fold(v):
        return jnp.sum(v.reshape(4, 8, 768), axis=0)

    for r0 in range(0, NR, 32):
        rows = slice(r0, r0 + 32)
        mk = mask_ref[rows, :]
        gm = mk * cot_ref[r0 // 8 : r0 // 8 + 4].astype(F32).reshape(32, 768)
        hv = hid[rows, :]
        out_ref[r0 // 8 : r0 // 8 + 4] = (mk * (hv + mix[rows, :] + fb)).reshape(4, 8, 768).astype(BF)
        c, rs = stats(hv)
        xh = c * rs
        gn = gn2[rows, :]
        e2 = gn * g2
        gh = gm + rs * (e2 - jnp.mean(e2, axis=-1, keepdims=True) - xh * jnp.mean(e2 * xh, axis=-1, keepdims=True))
        gb = mk * gh
        gh_ref[rows, :] = gh
        gbl[rows, :] = gb.astype(BF)
        for n, v in enumerate((gn * xh, gn, gb, gm)):
            sums[n] = sums[n] + fold(v)
    for n in range(4):
        vg_ref[n : n + 1, :] = jnp.sum(sums[n], axis=0, keepdims=True)
    tg_ref[...] = jnp.zeros_like(tg_ref)
    gn_ref[...] = jnp.zeros_like(gn_ref)

    def bwd_t(t, _):
        att_w = att[t]
        g_ref[0, t, :, 576:] = dotf(gbl[...], att_w, TN).astype(BF)
        proj[:NR, :192] = dotf(gbl[...], w_ref[0, t][:, 576:], NN)
        dqkv[...] = jnp.zeros_like(dqkv)
        for h in range(3):
            hh = 3 * t + h
            lo = 64 * h
            for w in range(3):
                rows = slice(w * WR, w * WR + WR) if w < 2 else slice(2 * WR, NR)
                dst = rows if w < 2 else slice(NR, NE)
                do = proj[rows, lo : lo + 64].astype(BF)
                p = probs[hh, rows, :]
                pf = p.astype(F32)
                dp = dotf(do, vals[hh, w], NT)
                delta = jnp.sum(pf * dp, axis=-1, keepdims=True)
                ds = (pf * (dp - delta)).astype(BF)
                dq = dotf(ds, kaug[hh, w], NN)
                qa = qaug[hh, rows, :]
                dqkv[dst, 192 + lo : 256 + lo] = dotf(ds, qa, TN)[:, :64].astype(BF)
                dqkv[dst, 384 + lo : 448 + lo] = dotf(p, do, TN).astype(BF)
                rel = jnp.take_along_axis(dq, back_ref[rows, :], axis=1, mode="promise_in_bounds").astype(BF)
                gq = dq[:, :64] * 0.125 + dotf(rel, tab_ref[...], NN)
                dqkv[rows, lo : lo + 64] = gq.astype(BF)
                tg_ref[...] += dotf(rel, qa, TN)[:64]
        vg_ref[pl.ds(12 + t, 1), 0:576] = jnp.sum(dqkv[...].astype(F32), axis=0, keepdims=True)
        g_ref[0, t, :, :576] = dotf(nrm[...], dqkv[...], TN).astype(BF)
        gn_ref[...] += dotf(dqkv[...], w_ref[0, t][:, :576], NT)
        return 0

    lax.fori_loop(0, 4, bwd_t, 0)


def compute(x, cot, mask, w, vec, qkvb, fc1b, ktail, fwd, back, tab, tabt):
    shp = jax.ShapeDtypeStruct
    vm = pl.BlockSpec(memory_space=pltpu.VMEM)
    return pl.pallas_call(
        compute_kernel,
        out_shape=(
            shp((NR // 8, 8, 768), BF), shp((NE, 768), F32), shp((NR, 768), F32), shp((3, 4, 768, 768), BF),
            shp((16, 768), F32), shp((64, 128), F32),
        ),
        in_specs=[vm] * 12,
        out_specs=(vm,) * 6,
        scratch_shapes=[
            pltpu.VMEM((NE, 768), BF), pltpu.VMEM((NE, 576), F32), pltpu.VMEM((HEADS, NR, 128), BF),
            pltpu.VMEM((HEADS, 3, WR, 128), BF), pltpu.VMEM((HEADS, 3, WR, 64), BF), pltpu.VMEM((HEADS, NR, WR), BF),
            pltpu.VMEM((4, NR, 192), BF), pltpu.VMEM((NR, 768), F32), pltpu.VMEM((NR, 768), BF),
            pltpu.VMEM((NR, 768), F32), pltpu.VMEM((NR, 768), F32), pltpu.VMEM((NR, 768), BF), pltpu.VMEM((NR, 768), BF),
            pltpu.VMEM((NR, 768), BF), pltpu.VMEM((NR, 768), BF), pltpu.VMEM((NE, 576), BF),
        ],
        compiler_params=pltpu.CompilerParams(vmem_limit_bytes=67043328),
    )(x, cot, mask, w, vec, qkvb, fc1b, ktail, fwd, back, tab, tabt)


MESH = pl.DeviceIdType.MESH


class Links:
    def __init__(self, send, recv):
        self.send, self.recv = send, recv
        self.x = lax.axis_index("dp")
        win = lax.axis_index("win")
        self.y, self.c = win // 2, win % 2
        self.z = lax.axis_index("tensor")
        self.xn = (1 - self.x, win, self.z)
        self.yn = (self.x, (1 - self.y) * 2 + self.c, self.z)
        self.sib = (self.x, self.y * 2 + 1 - self.c, self.z)
        self.win = win

    def zdev(self, z):
        return (self.x, self.win, z)

    def barrier(self):
        sem = pltpu.get_barrier_semaphore()
        others = [self.xn, self.yn, self.sib] + [self.zdev((self.z + d) % 4) for d in (1, 2, 3)]
        for dev in others:
            pl.semaphore_signal(sem, inc=1, device_id=dev, device_id_type=MESH)
        pl.semaphore_wait(sem, len(others))

    def copy(self, src, dst, n, dev):
        return pltpu.make_async_remote_copy(
            src_ref=src, dst_ref=dst, send_sem=self.send.at[n], recv_sem=self.recv.at[n], device_id=dev,
            device_id_type=MESH,
        )


AG_SEMS = 3 * 39


class Gather:
    def __init__(self, links, shard, w, local, base):
        self.l, self.shard, self.w, self.local, self.base = links, shard, w, local, base

    def sem(self, k, kind, i):
        start = {"z": 0, "x": 3, "y": 7, "hx": 11, "hy": 15, "so": 19, "sx": 23, "sy": 27, "sa": 31, "sb": 35}[kind]
        return self.base + k * 39 + start + i

    def rank(self, i):
        return (self.l.z + 4 - i) % 4

    def piece(self, k, i, px, py, c, half=None):
        ref = self.w.at[k, self.rank(i), px, py, c]
        return ref if half is None else ref.at[pl.ds(48 * half, 48)]

    def move(self, k, kind, i):
        l = self.l
        if kind == "z":
            src = self.shard.at[k]
            return l.copy(src, self.piece(k, 0, l.x, l.y, l.c), self.sem(k, kind, i - 1), l.zdev((l.z + i) % 4))
        px, py, half, dev = {
            "x": (l.x, l.y, None, l.xn), "y": (l.x, l.y, None, l.yn),
            "hx": (l.x, 1 - l.y, 1, l.xn), "hy": (1 - l.x, l.y, 0, l.yn),
            "so": (l.x, l.y, None, l.sib), "sx": (1 - l.x, l.y, None, l.sib), "sy": (l.x, 1 - l.y, None, l.sib),
            "sa": (1 - l.x, 1 - l.y, 0, l.sib), "sb": (1 - l.x, 1 - l.y, 1, l.sib),
        }[kind]
        dst = self.piece(k, i, px, py, l.c, half)
        own = kind in ("x", "y", "so") and i == 0
        return l.copy(self.shard.at[k] if own else dst, dst, self.sem(k, kind, i), dev)

    def start(self, k, kind, i):
        self.move(k, kind, i).start()

    def arrived(self, k, kind, i):
        self.move(k, kind, i).wait_recv()

    def own(self, k):
        l = self.l
        pltpu.make_async_copy(self.shard.at[k], self.piece(k, 0, l.x, l.y, l.c), self.local.at[k]).start()
        for i in (1, 3, 2):
            self.start(k, "z", i)
        for kind in ("x", "y", "so"):
            self.start(k, kind, 0)

    def along(self, k, i):
        self.arrived(k, "z", i)
        for kind in ("x", "y", "so"):
            self.start(k, kind, i)

    def across(self, k, i):
        self.arrived(k, "x", i)
        self.start(k, "hy", i)
        self.start(k, "sx", i)
        self.arrived(k, "y", i)
        self.start(k, "hx", i)
        self.start(k, "sy", i)

    def corner(self, k, i):
        self.arrived(k, "hy", i)
        self.start(k, "sa", i)
        self.arrived(k, "hx", i)
        self.start(k, "sb", i)

    def partner(self, k):
        l = self.l
        for i in range(4):
            for kind in ("so", "sx", "sy", "sa", "sb"):
                self.arrived(k, kind, i)
        pltpu.make_async_copy(self.shard.at[k], self.piece(k, 0, l.x, l.y, l.c), self.local.at[k]).wait()

    def drain(self):
        for k in range(3):
            for i in (1, 2, 3):
                self.move(k, "z", i).wait_send()
            for kind in ("x", "y", "hx", "hy", "so", "sx", "sy", "sa", "sb"):
                for i in range(4):
                    self.move(k, kind, i).wait_send()


RS_SEMS = 12 * 6


class Scatter:
    def __init__(self, links, g, r1, r2, r3, r4, base):
        self.l, self.g, self.r1, self.r2, self.r3, self.r4, self.base = links, g, r1, r2, r3, r4, base

    def moves(self, n, stage):
        l, s = self.l, self.base + 6 * n
        g = self.g(n)
        if stage == 1:
            return [l.copy(g.at[:, :, 1 - l.c], self.r1.at[n], s, l.sib)]
        if stage == 2:
            return [
                l.copy(g.at[:, 1 - l.y, l.c, 0:48], self.r2.at[n, 0], s + 1, l.yn),
                l.copy(g.at[1 - l.x, :, l.c, 48:96], self.r2.at[n, 1], s + 2, l.xn),
            ]
        return [
            l.copy(g.at[1 - l.x, l.y, l.c, 0:48], self.r3.at[n, 0], s + 3, l.xn),
            l.copy(g.at[l.x, 1 - l.y, l.c, 48:96], self.r3.at[n, 1], s + 4, l.yn),
        ]

    def start(self, n, stage):
        for m in self.moves(n, stage):
            m.start()

    def wait(self, n, stage):
        for m in self.moves(n, stage):
            m.wait_recv()

    def last(self, n, k, d):
        l, g = self.l, self.g(n)
        return l.copy(g.at[l.x, l.y, l.c], self.r4.at[k, d - 1], self.base + 6 * n + 5, l.zdev((l.z + d) % 4))

    def add1(self, n):
        l, g = self.l, self.g(n)
        for a in range(2):
            for b in range(2):
                ref = g.at[a, b, l.c]
                ref[...] = ref[...] + self.r1[n, a, b]

    def add2(self, n):
        l, g = self.l, self.g(n)
        for a in range(2):
            ref = g.at[a, l.y, l.c, 0:48]
            ref[...] = ref[...] + self.r2[n, 0, a]
            ref = g.at[l.x, a, l.c, 48:96]
            ref[...] = ref[...] + self.r2[n, 1, a]

    def add3(self, n):
        l, g = self.l, self.g(n)
        for h in range(2):
            ref = g.at[l.x, l.y, l.c, pl.ds(48 * h, 48)]
            ref[...] = ref[...] + self.r3[n, h]


class Rows:
    TABLE = block_table()

    def __init__(self, links, local):
        self.l, self.local = links, local

    @staticmethod
    def home(block):
        m, b = divmod(int(block), 12)
        return b // 3, m * 3 + b % 3

    @staticmethod
    def unit(slot):
        return 7 * slot if slot < 9 else NR // 8 + 7 * (slot - 9)

    def inward(self, held, rows, slots, base, do):
        l = self.l
        for me in range(4):

            @pl.when(l.z == me)
            def _():
                sent = 0
                for slot in range(slots):
                    for step in range(4):
                        dev = (me + step) % 4
                        owner, idx = self.home(self.TABLE[dev, slot])
                        if owner != me:
                            continue
                        dst = rows.at[pl.ds(self.unit(slot), 7)]
                        if dev == me:
                            if do != "drain":
                                c = pltpu.make_async_copy(held.at[idx], dst, self.local.at[base + slot])
                                c.start() if do == "start" else c.wait()
                            continue
                        sent += 1
                        if do == "wait":
                            continue
                        c = pltpu.make_async_remote_copy(
                            src_ref=held.at[idx], dst_ref=dst, send_sem=l.send.at[base + sent - 1],
                            recv_sem=l.recv.at[base + slot], device_id=l.zdev(dev), device_id_type=MESH,
                        )
                        c.start() if do == "start" else c.wait_send()
                    owner, idx = self.home(self.TABLE[me, slot])
                    if do == "wait" and owner != me:
                        pltpu.make_async_remote_copy(
                            src_ref=held.at[0], dst_ref=rows.at[pl.ds(self.unit(slot), 7)], send_sem=l.send.at[base],
                            recv_sem=l.recv.at[base + slot], device_id=l.zdev(owner), device_id_type=MESH,
                        ).wait_recv()

    def outward(self, rows, held, base, do):
        l = self.l
        for me in range(4):

            @pl.when(l.z == me)
            def _():
                for slot in range(9):
                    owner, idx = self.home(self.TABLE[me, slot])
                    src = rows.at[pl.ds(7 * slot, 7)]
                    if owner == me:
                        if do != "drain":
                            c = pltpu.make_async_copy(src, held.at[idx], self.local.at[base + slot])
                            c.start() if do == "start" else c.wait()
                    elif do != "wait":
                        c = pltpu.make_async_remote_copy(
                            src_ref=src, dst_ref=held.at[idx], send_sem=l.send.at[base + slot],
                            recv_sem=l.recv.at[base + idx], device_id=l.zdev(owner), device_id_type=MESH,
                        )
                        c.start() if do == "start" else c.wait_send()
                for dev in range(4):
                    for slot in range(9):
                        owner, idx = self.home(self.TABLE[dev, slot])
                        if do == "wait" and owner == me and dev != me:
                            pltpu.make_async_remote_copy(
                                src_ref=rows.at[pl.ds(0, 7)], dst_ref=held.at[idx], send_sem=l.send.at[base],
                                recv_sem=l.recv.at[base + idx], device_id=l.zdev(dev), device_id_type=MESH,
                            ).wait_recv()


XS, CS, GS = 0, 13, 13 + 9
AG0 = GS + 9


def gather_kernel(x_in, cot_in, shard, x, cot, w, send, recv, local):
    x[63] = jnp.zeros((8, 768), BF)
    cot[63] = jnp.zeros((8, 768), BF)
    links = Links(send, recv)
    links.barrier()
    rows = Rows(links, local)
    ag = Gather(links, shard, w, local.at[pl.ds(40, 3)], AG0)
    rows.inward(x_in, x, 13, XS, "start")
    ag.own(0)
    rows.inward(cot_in, cot, 9, CS, "start")
    order = [("along", 0), ("own", 1), ("across", 0), ("along", 1), ("own", 2), ("corner", 0), ("across", 1), ("along", 2),
             ("corner", 1), ("across", 2), ("corner", 2)]
    for kind, k in order:
        if kind == "own":
            ag.own(k)
        else:
            for i in (range(1, 4) if kind == "along" else range(4)):
                getattr(ag, kind)(k, i)
    for k in range(3):
        ag.partner(k)
    rows.inward(x_in, x, 13, XS, "wait")
    rows.inward(cot_in, cot, 9, CS, "wait")
    rows.inward(x_in, x, 13, XS, "drain")
    rows.inward(cot_in, cot, 9, CS, "drain")
    ag.drain()


def gather_call(xh, coth, shard):
    shp = jax.ShapeDtypeStruct
    vm = pl.BlockSpec(memory_space=pltpu.VMEM)
    n = AG0 + AG_SEMS
    return pl.pallas_call(
        gather_kernel,
        out_shape=(shp((NE // 8, 8, 768), BF), shp((NR // 8, 8, 768), BF), shp((3, 4, 2, 2, 2, 96, 768), BF)),
        in_specs=[vm] * 3,
        out_specs=(vm,) * 3,
        scratch_shapes=[pltpu.SemaphoreType.DMA((n,)), pltpu.SemaphoreType.DMA((n,)), pltpu.SemaphoreType.DMA((48,))],
        compiler_params=pltpu.CompilerParams(collective_id=0, has_side_effects=True, vmem_limit_bytes=67043328),
    )(xh, coth, shard)


RET0 = 0
DX0 = 9
SH0 = 18
VS0 = 21
RS0 = VS0 + 10


def scatter_kernel(g_in, x, mask_ref, gain_ref, gn_ref, gh_ref, vg_in, tg_in, out,
                   own, out_h, dx_h, vg_out, tg_out,
                   g, r1, r2, r3, r4, gs, gsr, dx, vg, tg, vr, tr, send, recv, local):
    links = Links(send, recv)
    for n in range(12):
        pltpu.make_async_copy(g_in.at[n // 4, (links.z + n % 4 + 1) % 4], g.at[n], local.at[20 + n]).start()
    links.barrier()
    rows = Rows(links, local)
    rs = Scatter(links, lambda n: g.at[n], r1, r2, r3, r4, RS0)
    rows.outward(out, out_h, RET0, "start")
    gs[...] = gn_ref[NR:].reshape(WR // 8, 8, 768).astype(BF)
    sh = [
        links.copy(gs.at[pl.ds(7 * ((links.z + d) % 4), 7)], gsr.at[d - 1], SH0 + d - 1, links.zdev((links.z + d) % 4))
        for d in (1, 2, 3)
    ]
    for c in sh:
        c.start()

    for n in range(12):
        pltpu.make_async_copy(g_in.at[n // 4, (links.z + n % 4 + 1) % 4], g.at[n], local.at[20 + n]).wait()
        rs.start(n, 1)
    for c in sh:
        c.wait_recv()
    first_norm_back(links, x, mask_ref, gain_ref, gn_ref, gh_ref, gs, gsr, dx, vg_in, vg.at[0])
    rows.outward(dx, dx_h, DX0, "start")
    tg[0] = tg_in[...]
    for n in range(12):
        rs.wait(n, 1)
        rs.add1(n)
        rs.start(n, 2)
    for n in range(12):
        rs.wait(n, 2)
        rs.add2(n)
        rs.start(n, 3)
    for n in range(12):
        rs.wait(n, 3)
        rs.add3(n)
        if n % 4 < 3:
            rs.last(n, n // 4, n % 4 + 1).start()
    small_sums(links, vg, tg, vr, tr)
    vg_out[...] = vg[5]
    tg_out[...] = tg[5]
    for k in range(3):
        for d in (1, 2, 3):
            rs.last(4 * k + d - 1, k, d).wait_recv()
        fin = g[4 * k + 3, links.x, links.y, links.c].astype(F32)
        for d in range(3):
            fin = fin + r4[k, d].astype(F32)
        own[k] = fin
    rows.outward(out, out_h, RET0, "wait")
    rows.outward(dx, dx_h, DX0, "wait")
    rows.outward(out, out_h, RET0, "drain")
    rows.outward(dx, dx_h, DX0, "drain")
    for c in sh:
        c.wait_send()
    for n in range(12):
        for stage in (1, 2, 3):
            for m in rs.moves(n, stage):
                m.wait_send()
        if n % 4 < 3:
            rs.last(n, n // 4, n % 4 + 1).wait_send()


def first_norm_back(links, x, mask_ref, gain_ref, gn_ref, gh_ref, gs, gsr, dx, vg_in, vg):
    own = gn_ref[pl.ds(pl.multiple_of(NR + 56 * links.z, 8), 56), :]
    for d in range(3):
        own = own + gsr[d].astype(F32).reshape(56, 768)
    quarter = gn_ref[2 * WR : 2 * WR + 56, :] + own
    g1 = gain_ref[0:1, :]
    s_gain = jnp.zeros((8, 768), F32)
    s_bias = jnp.zeros((8, 768), F32)
    for r0, n in [(r, 32) for r in range(0, 2 * WR, 32)] + [(2 * WR, 56)]:
        rows = slice(r0, r0 + n)
        v = x[r0 // 8 : (r0 + n) // 8].astype(F32).reshape(n, 768)
        c = v - jnp.mean(v, axis=-1, keepdims=True)
        rs = lax.rsqrt(jnp.mean(c * c, axis=-1, keepdims=True) + 1e-6)
        xh = c * rs
        gn = mask_ref[rows, :] * (gn_ref[rows, :] if n == 32 else quarter)
        e1 = gn * g1
        gx = gh_ref[rows, :] + rs * (
            e1 - jnp.mean(e1, axis=-1, keepdims=True) - xh * jnp.mean(e1 * xh, axis=-1, keepdims=True)
        )
        dx[r0 // 8 : (r0 + n) // 8] = gx.reshape(n // 8, 8, 768).astype(BF)
        s_gain = s_gain + jnp.sum((gn * xh).reshape(n // 8, 8, 768), axis=0)
        s_bias = s_bias + jnp.sum(gn.reshape(n // 8, 8, 768), axis=0)
    vg[...] = vg_in[...]
    vg[4:5, :] = jnp.sum(s_gain, axis=0, keepdims=True)
    vg[5:6, :] = jnp.sum(s_bias, axis=0, keepdims=True)


def small_sums(links, vg, tg, vr, tr):
    l = links
    partners = [l.sib, l.xn, l.yn, l.zdev((l.z // 2) * 2 + 1 - l.z % 2), l.zdev((l.z + 2) % 4)]
    copies = []
    for n, dev in enumerate(partners):
        pair = [l.copy(vg.at[n], vr.at[n], VS0 + 2 * n, dev), l.copy(tg.at[n], tr.at[n], VS0 + 2 * n + 1, dev)]
        for c in pair:
            c.start()
        for c in pair:
            c.wait_recv()
        vg[n + 1] = vg[n] + vr[n]
        tg[n + 1] = tg[n] + tr[n]
        copies += pair
    for c in copies:
        c.wait_send()


def scatter_call(grads, x, mask, vec, gn, gh, vg, tg, out):
    shp = jax.ShapeDtypeStruct
    vm = pl.BlockSpec(memory_space=pltpu.VMEM)
    n = RS0 + RS_SEMS
    return pl.pallas_call(
        scatter_kernel,
        out_shape=(
            shp((3, 96, 768), F32), shp((9, 7, 8, 768), BF), shp((9, 7, 8, 768), BF), shp((16, 768), F32), shp((64, 128), F32),
        ),
        in_specs=[pl.BlockSpec(memory_space=pl.ANY)] + [vm] * 8,
        out_specs=(vm,) * 5,
        scratch_shapes=[
            pltpu.VMEM((12, 2, 2, 2, 96, 768), BF), pltpu.VMEM((12, 2, 2, 96, 768), BF), pltpu.VMEM((12, 2, 2, 48, 768), BF),
            pltpu.VMEM((12, 2, 48, 768), BF), pltpu.VMEM((3, 3, 96, 768), BF), pltpu.VMEM((WR // 8, 8, 768), BF),
            pltpu.VMEM((3, 7, 8, 768), BF), pltpu.VMEM((NR // 8, 8, 768), BF), pltpu.VMEM((6, 16, 768), F32),
            pltpu.VMEM((6, 64, 128), F32), pltpu.VMEM((5, 16, 768), F32), pltpu.VMEM((5, 64, 128), F32),
            pltpu.SemaphoreType.DMA((n,)), pltpu.SemaphoreType.DMA((n,)), pltpu.SemaphoreType.DMA((32,)),
        ],
        compiler_params=pltpu.CompilerParams(collective_id=1, has_side_effects=True, vmem_limit_bytes=67043328),
    )(grads, x, mask, vec, gn, gh, vg, tg, out)


def plain_gather(xh, coth, shard):
    mine = lax.dynamic_index_in_dim(jnp.asarray(block_table()), lax.axis_index("tensor"), 0, keepdims=False)

    def spread(held, count):
        blocks = lax.all_gather(held.reshape(3, 3, 7, 8, 768), "tensor", axis=1).reshape(36, 7, 8, 768)
        got = jnp.take(blocks, mine[:count], axis=0).reshape(-1, 8, 768)
        return jnp.concatenate([got[:63], jnp.zeros((1, 8, 768), BF), got[63:]], axis=0)

    whole = lax.all_gather(lax.all_gather(shard, ("dp", "win"), axis=1, tiled=True), "tensor", axis=1)
    return spread(xh, 13), spread(coth, 9), whole


def plain_scatter(grads, x, mask, vec, gn, gh, vg, tg, out):
    shared = lax.psum_scatter(gn[NR:], "tensor", scatter_dimension=0, tiled=True)
    gn = mask * (gn[:NR] + jnp.pad(shared, ((2 * WR, QR - BP), (0, 0))))
    xf = x[: NR // 8].reshape(NR, 768).astype(F32)
    cen = xf - jnp.mean(xf, axis=-1, keepdims=True)
    rs = lax.rsqrt(jnp.mean(cen * cen, axis=-1, keepdims=True) + 1e-6)
    xh = cen * rs
    e1 = gn * vec[0]
    gx = gh + rs * (e1 - jnp.mean(e1, axis=-1, keepdims=True) - xh * jnp.mean(e1 * xh, axis=-1, keepdims=True))
    vg = vg.at[4].set(jnp.sum(gn * xh, axis=0)).at[5].set(jnp.sum(gn, axis=0))
    back_to = lax.dynamic_index_in_dim(jnp.asarray(home_table()), lax.axis_index("tensor"), 0, keepdims=False)

    def bring(rows):
        blocks = lax.all_gather(rows[:63].reshape(9, 7, 8, 768), "tensor", axis=0, tiled=True)
        return jnp.take(blocks, back_to, axis=0)

    own = lax.psum_scatter(grads.reshape(3, 4, 768, 768), "tensor", scatter_dimension=1, tiled=False)
    own = lax.psum_scatter(own, ("dp", "win"), scatter_dimension=1, tiled=True).astype(F32)
    vg, tg = lax.psum((vg, tg), ("dp", "win", "tensor"))
    return own, bring(out), bring(gx.astype(BF).reshape(NR // 8, 8, 768)), vg, tg


def per_device(
    links, tokens, window_ids, norm1_gain, norm1_bias, qkv_weight, qv_bias, rel_height, rel_width, proj_weight, proj_bias,
    norm2_gain, norm2_bias, fc1_weight, fc1_bias, fc2_weight, fc2_bias, out_grad,
):
    rank = lax.axis_index("tensor")

    def home_blocks(rows):
        return jnp.pad(rows.reshape(9, BT, 768), ((0, 0), (0, BP - BT), (0, 0))).reshape(9, 7, 8, 768)

    shard = jnp.stack(
        [
            jnp.concatenate([qkv_weight.reshape(-1, 576), proj_weight.T], axis=1),
            fc1_weight,
            fc2_weight.T,
        ]
    )
    x, cot, whole = (gather_call if links else plain_gather)(home_blocks(tokens), home_blocks(out_grad), shard)
    whole = whole.reshape(3, 4, 768, 768)

    wi, wj, wv = token_positions()
    wi, wj, wv = jnp.asarray(wi, jnp.int32), jnp.asarray(wj, jnp.int32), jnp.asarray(wv)
    qi = jnp.pad(lax.dynamic_slice_in_dim(wi, rank * BP, BP), (0, QR - BP))
    qj = jnp.pad(lax.dynamic_slice_in_dim(wj, rank * BP, BP), (0, QR - BP))
    qv = jnp.pad(lax.dynamic_slice_in_dim(wv, rank * BP, BP), (0, QR - BP))
    ids = window_ids.reshape(9)
    slots = jnp.asarray([[m * 3 + s for m, s in WINDOWS_OF[dev]] + [4, 4] for dev in range(4)], jnp.int32)
    wid = jnp.take(ids, lax.dynamic_index_in_dim(slots, rank, 0, keepdims=False), axis=0)

    across = (GRID + WS - 1) // WS

    def valid(w, i, j, ok):
        return ok & (w < across * across) & ((w // across) * WS + i < GRID) & ((w % across) * WS + j < GRID)

    mask = jnp.concatenate(
        [valid(wid[0], wi, wj, wv), valid(wid[1], wi, wj, wv), valid(wid[2], qi, qj, qv), valid(wid[3], wi, wj, wv)]
    ).astype(F32)[:, None]
    ii = jnp.concatenate([wi, wi, qi])
    jj = jnp.concatenate([wj, wj, qj])
    fwd, back = pick_lanes(ii, jj)

    small = jnp.concatenate(
        [fc1_bias[None], jnp.pad(qv_bias.reshape(1, 384), ((0, 0), (0, 384))), jnp.zeros((14, 768), BF)], axis=0
    )
    small = lax.all_gather(small, "tensor", axis=0).astype(F32)
    fc1b = small[:, 0:1, :]
    qkvb = jnp.concatenate([small[:, 1:2, :192], jnp.zeros((4, 1, 192), F32), small[:, 1:2, 192:384]], axis=2)
    vec = jnp.stack(
        [norm1_gain, norm1_bias, proj_bias, norm2_gain, norm2_bias, fc2_bias, fc2_bias, fc2_bias]
    ).astype(F32)
    tab = jnp.zeros((128, 64), BF).at[0:27].set(rel_height).at[32:59].set(rel_width)
    tabt = (tab * BF(8)).T
    ktail = jnp.asarray(key_tail(), BF)

    out, gn, gh, grads, vg, tg = compute(x, cot, mask, whole, vec, qkvb, fc1b, ktail, fwd, back, tab, tabt)
    own, out, dx, vg, tg = (scatter_call if links else plain_scatter)(
        grads.reshape(3, 4, 2, 2, 2, 96, 768), x, mask[:NR], vec, gn, gh, vg, tg, out
    )

    def tokens_of(blocks):
        return blocks.reshape(9, BP, 768)[:, :BT].reshape(tokens.shape)

    output = tokens_of(out)
    grad_tokens = tokens_of(dx).astype(F32)
    g_qkv = own[0, :, :576].reshape(qkv_weight.shape)
    g_proj = own[0, :, 576:].T
    g_fc1 = own[1]
    g_fc2 = own[2].T
    g_qv = jnp.stack([vg[12:16, :192].reshape(-1), vg[12:16, 384:576].reshape(-1)])
    return (
        output, grad_tokens, vg[4], vg[5], g_qkv, g_qv, tg[0:27, :64] * 8.0, tg[32:59, :64] * 8.0, g_proj,
        vg[2], vg[0], vg[1], g_fc1, vg[8:12].reshape(-1), g_fc2, vg[3],
    )


def solution(mesh):
    in_specs = (
        P("dp", "win", "tensor", None), P("dp", "win", None), P(), P(), P(("dp", "win"), None, "tensor"),
        P(None, "tensor"), P(), P(), P("tensor", ("dp", "win")), P(), P(), P(), P(("dp", "win"), "tensor"), P("tensor"),
        P("tensor", ("dp", "win")), P(), P("dp", "win", "tensor", None),
    )
    out_specs = (
        P("dp", "win", "tensor", None), P("dp", "win", "tensor", None), P(), P(), P(("dp", "win"), None, "tensor"), P(),
        P(), P(), P("tensor", ("dp", "win")), P(), P(), P(), P(("dp", "win"), "tensor"), P(),
        P("tensor", ("dp", "win")), P(),
    )
    links = dict(mesh.shape) == {"dp": 2, "win": 4, "tensor": 4}
    return jax.shard_map(partial(per_device, links), mesh=mesh, in_specs=in_specs, out_specs=out_specs, check_vma=False)
```

time: 1550 us -> 338 us (0.22)
  blocking collectives: 635 us -> 13.4 us
  Pallas kernels: 0 us -> 276 us
  local copies, waits for them, and re-layouts: 292 us -> 24.9 us
  waiting for transfers between devices: 249 us -> 0 us
  matrix products: 205 us -> 0 us
  other arithmetic: 107 us -> 11.7 us
  starting transfers between devices: 31.2 us -> 0 us
    while x9 -> x0, blocking collectives: 295 us -> none
    all_gather x18 -> x1, blocking collectives: 299 us -> 13.4 us  [per_device(): small = lax.all_gather(small, 'tensor', axis=0).astype(F32)]
    pallas_call x0 -> x3, Pallas kernels: none -> 276 us  [the longest x1 105 us: scatter_call(): pl.pallas_call(scatter_kernel, out_shape=(shp((3, 96, 768), F32), shp((9,...]
    reduce_scatter x9 -> x0, waiting for transfers between devices: 245 us -> none  [the longest x3 134 us: run_block(): lax.psum_scatter(local_big[2], ('dp', 'win'), scatter_dimension=0, tiled=...]
    dot_general x69 -> x0, matrix products: 194 us -> none  [the longest x3 25.4 us: run_block(): jnp.einsum('rd,fd->rf', grad_mixed_all, fc2_full, preferred_element_type=...]
    reshape x25 -> x8, local copies, waits for them, and re-layouts: 121 us -> 4.21 us  [the longest x1 1.24 us: home_blocks(): jnp.pad(rows.reshape(9, BT, 768), ((0, 0), (0, BP - BT), (0, 0)))]
    while x411 -> x0, local copies, waits for them, and re-layouts: 79.5 us -> none
    reduce_sum x30 -> x0, other arithmetic: 59 us -> none  [the longest x3 27.2 us: run_block(): jnp.sum(jnp.exp(scores - top_score), axis=-1, keepdims=True)]
  transfers between devices with their start and end apart: 30 -> 0, of which waited for: 9 -> 0; matrix products, arithmetic and copies ran while one was open for 38% -> 0% of each run, Pallas kernels for 0% -> 0%
where the time goes in v1:
time: 338 us; the launch traced here: 337 us
  Pallas kernels  276 us (82%)
  local copies, waits for them, and re-layouts  24.9 us (7%)
  blocking collectives  13.4 us (4%)
  other arithmetic  11.7 us (3%)
  between operations  11.3 us (3%)
    pallas_call x1, Pallas kernels, scatter_call(): pl.pallas_call(scatter_kernel, out_shape=(shp((3, 96, 768), F32), shp((9,...  105 us
    pallas_call x1, Pallas kernels, gather_call(): pl.pallas_call(gather_kernel, out_shape=(shp((NE // 8, 8, 768), BF), shp(...  93.2 us
    pallas_call x1, Pallas kernels, compute(): pl.pallas_call(compute_kernel, out_shape=(shp((NR // 8, 8, 768), BF), shp...  77.9 us
    all_gather x1, blocking collectives, per_device(): small = lax.all_gather(small, 'tensor', axis=0).astype(F32)  13.4 us

profile of v1, /device:TPU:0, one launch (start us, length us, event | category | flops | bytes accessed | tf_op | source)
XLA Modules:
  0.0 337.2 jit_solution(7632108714301291706)
XLA Ops:
  0.7 0.8 fusion.11
  15.4 0.8 dynamic_slice.15
  16.1 0.8 dynamic_slice.16
  16.9 0.7 dynamic_slice.14
  17.7 0.9 copy.85.mask_ref
  18.7 0.8 pad_add_fusion
  19.5 1.8 add_select_fusion
  21.8 1.2 pad_bitcast_fusion
  23.6 0.8 pad_maximum_fusion.shard
  24.4 93.2 %shard_map.414 = (bf16[92,8,768]{2,1,0:T(8,128)(2,1)}, bf16[64,8,768]{2,1,0:T(8,128)(2,1)}, bf16[3,4,2,2,2,96,768]{6,5,4,3,2,1,0:T(8,128)(2,1)}) custom-call(bf16[9,7,8,768]{3,2,1,0:T(8,128)(2,1)} %get-tuple-element.158.x_in, bf16[9,7,8,768]{3,2,1,0:T(8,128)(2,1)} %get-tuple-element.157.cot_in, bf16[3,96,768]{2,1,0:T(8,128)(2,1)} %pad_maximum_fusion.shard), custom_call_target="tpu_custom_call" | custom-call | tf_op jit(solution)/shard_map/pallas_call | solution.py:546
  118.3 0.8 reshape.294
  119.2 13.4 %all-gather = bf16[64,768]{1,0:T(8,128)(2,1)S(1)} all-gather(bf16[16,768]{1,0:T(8,128)(2,1)S(1)} %fusion.10), channel_id=2, replica_groups=mesh['dp'=2,'win'=4,'tensor'=4] {'tensor'}, dimensions={0}, use_global_device_ids=true | all-gather | bytes 122880 | tf_op jit(solution)/shard_map/all_gather | solution.py:769
  134.0 0.8 copy.83
  134.8 0.8 copy.84
  142.1 77.9 %shard_map.415 = (bf16[64,8,768]{2,1,0:T(8,128)(2,1)}, f32[736,768]{1,0:T(8,128)}, f32[512,768]{1,0:T(8,128)}, bf16[3,4,768,768]{3,2,1,0:T(8,128)(2,1)}, f32[16,768]{1,0:T(8,128)}, /*index=5*/f32[64,128]{1,0:T(8,128)}) custom-call(bf16[92,8,768]{2,1,0:T(8,128)(2,1)} %get-tuple-element.54.x_ref.x, bf16[64,8,768]{2,1,0:T(8,128)(2,1)} %get-tuple-element.55.cot_ref, ...), custom_call_target="tpu_custom_call" | custom-call | tf_op jit(solution)/shard_map/pallas_call | solution.py:244
  220.0 0.8 add_convert_fusion.1
  220.7 0.9 copy.87.mask_ref
  221.6 104.8 %shard_map.416 = (f32[3,96,768]{2,1,0:T(8,128)}, bf16[9,7,8,768]{3,2,1,0:T(8,128)(2,1)}, bf16[9,7,8,768]{3,2,1,0:T(8,128)(2,1)}, f32[16,768]{1,0:T(8,128)}, f32[64,128]{1,0:T(8,128)}) custom-call(bf16[3,4,2,2,2,96,768]{6,5,4,3,2,1,0:T(8,128)(2,1)} %bitcast.57, bf16[92,8,768]{2,1,0:T(8,128)(2,1)} %get-tuple-element.54.x_ref.x, f32[512,1]{1,0:T(8,128)} %copy.87.mask_ref, ...), custom_call_target="tpu_custom_call" | custom-call | tf_op jit(solution)/shard_map/pallas_call | solution.py:674
  327.8 1.2 slice_convert_fusion
  329.1 2.5 reshape.301
  331.8 0.9 copy.89
  332.6 1.0 reshape.297
  333.7 0.8 slice_bitcast_fusion
  334.6 0.7 copy.90
  (78 shorter events, 16.7 us)
Async XLA Ops:
  0.6 20.7 %copy-start.2 = (bf16[1,3,147,768]{3,2,1,0:T(8,128)(2,1)S(1)}, bf16[1,3,147,768]{3,2,1,0:T(8,128)(2,1)}, u32[]{:S(2)}) copy-start(bf16[1,3,147,768]{3,2,1,0:T(8,128)(2,1)} %param.35) | copy-start | bytes 2032132
  2.2 19.3 %copy-start.3 = (bf16[1,3,147,768]{3,2,1,0:T(8,128)(2,1)S(1)}, bf16[1,3,147,768]{3,2,1,0:T(8,128)(2,1)}, u32[]{:S(2)}) copy-start(bf16[1,3,147,768]{3,2,1,0:T(8,128)(2,1)} %param.51) | copy-start | bytes 2032132
  12.7 4.2 %copy-start.12 = (pred[224]{0:T(512)(128)(4,1)}, pred[224]{0:T(512)(128)(4,1)S(1)}, u32[]{:S(2)}) copy-start(pred[224]{0:T(512)(128)(4,1)S(1)} %get-tuple-element.147) | copy-start | bytes 676
  12.7 4.9 %copy-start.11 = (pred[224]{0:T(512)(128)(4,1)}, pred[224]{0:T(512)(128)(4,1)S(1)}, u32[]{:S(2)}) copy-start(pred[224]{0:T(512)(128)(4,1)S(1)} %get-tuple-element.146) | copy-start | bytes 676
  17.7 1.0 copy-start.10
  21.7 1.3 copy-start.6
  21.7 1.6 copy-start.7
  21.8 1.8 copy-start.4
  21.8 1.8 copy-start.5
  329.1 2.5 copy-start
  329.1 3.6 %copy-start.1 = (bf16[9,7,8,768]{3,2,1,0:T(8,128)(2,1)S(1)}, bf16[9,7,8,768]{3,2,1,0:T(8,128)(2,1)}, u32[]{:S(2)}) copy-start(bf16[9,7,8,768]{3,2,1,0:T(8,128)(2,1)} %get-tuple-element.63) | copy-start | bytes 2322436
  332.6 2.7 copy-start.8
  332.6 3.3 copy-start.9

commit v2 on v1

--- a/solution.py
+++ b/solution.py
@@ -331,16 +331,19 @@
     def arrived(self, k, kind, i):
         self.move(k, kind, i).wait_recv()
 
-    def own(self, k):
+    def keep(self, k):
         l = self.l
-        pltpu.make_async_copy(self.shard.at[k], self.piece(k, 0, l.x, l.y, l.c), self.local.at[k]).start()
+        return pltpu.make_async_copy(self.shard.at[k], self.piece(k, 0, l.x, l.y, l.c), self.local.at[k])
+
+    def own_z(self, k):
         for i in (1, 3, 2):
             self.start(k, "z", i)
-        for kind in ("x", "y", "so"):
-            self.start(k, kind, 0)
 
     def along(self, k, i):
-        self.arrived(k, "z", i)
+        if i:
+            self.arrived(k, "z", i)
+        else:
+            self.keep(k).start()
         for kind in ("x", "y", "so"):
             self.start(k, kind, i)
 
@@ -358,32 +361,31 @@
         self.arrived(k, "hx", i)
         self.start(k, "sb", i)
 
-    def partner(self, k):
-        l = self.l
-        for i in range(4):
-            for kind in ("so", "sx", "sy", "sa", "sb"):
-                self.arrived(k, kind, i)
-        pltpu.make_async_copy(self.shard.at[k], self.piece(k, 0, l.x, l.y, l.c), self.local.at[k]).wait()
-
-    def drain(self):
-        for k in range(3):
-            for i in (1, 2, 3):
-                self.move(k, "z", i).wait_send()
-            for kind in ("x", "y", "hx", "hy", "so", "sx", "sy", "sa", "sb"):
-                for i in range(4):
-                    self.move(k, kind, i).wait_send()
+    def partner(self, k, i):
+        for kind in ("so", "sx", "sy", "sa", "sb"):
+            self.arrived(k, kind, i)
+        if not i:
+            self.keep(k).wait()
+
+    def drain(self, k, i):
+        for kind in ("x", "y", "hx", "hy", "so", "sx", "sy", "sa", "sb"):
+            self.move(k, kind, i).wait_send()
 
 
 RS_SEMS = 12 * 6
 
 
 class Scatter:
-    def __init__(self, links, g, r1, r2, r3, r4, base):
-        self.l, self.g, self.r1, self.r2, self.r3, self.r4, self.base = links, g, r1, r2, r3, r4, base
-
-    def moves(self, n, stage):
-        l, s = self.l, self.base + 6 * n
-        g = self.g(n)
+    def __init__(self, links, w, r1, r2, r3, r4, base):
+        self.l, self.w, self.r1, self.r2, self.r3, self.r4, self.base = links, w, r1, r2, r3, r4, base
+
+    def g(self, k, i):
+        return self.w.at[k, (self.l.z + 4 - i) % 4]
+
+    def moves(self, k, i, stage):
+        l, n = self.l, 4 * k + i
+        s = self.base + 6 * n
+        g = self.g(k, i)
         if stage == 1:
             return [l.copy(g.at[:, :, 1 - l.c], self.r1.at[n], s, l.sib)]
         if stage == 2:
@@ -391,43 +393,55 @@
                 l.copy(g.at[:, 1 - l.y, l.c, 0:48], self.r2.at[n, 0], s + 1, l.yn),
                 l.copy(g.at[1 - l.x, :, l.c, 48:96], self.r2.at[n, 1], s + 2, l.xn),
             ]
-        return [
-            l.copy(g.at[1 - l.x, l.y, l.c, 0:48], self.r3.at[n, 0], s + 3, l.xn),
-            l.copy(g.at[l.x, 1 - l.y, l.c, 48:96], self.r3.at[n, 1], s + 4, l.yn),
-        ]
-
-    def start(self, n, stage):
-        for m in self.moves(n, stage):
+        if stage == 3:
+            return [
+                l.copy(g.at[1 - l.x, l.y, l.c, 0:48], self.r3.at[n, 0], s + 3, l.xn),
+                l.copy(g.at[l.x, 1 - l.y, l.c, 48:96], self.r3.at[n, 1], s + 4, l.yn),
+            ]
+        return [l.copy(g.at[l.x, l.y, l.c], self.r4.at[k, i - 1], s + 5, l.zdev((l.z + 4 - i) % 4))] if i else []
+
+    def start(self, k, i, stage):
+        for m in self.moves(k, i, stage):
             m.start()
 
-    def wait(self, n, stage):
-        for m in self.moves(n, stage):
+    def wait(self, k, i, stage):
+        for m in self.moves(k, i, stage):
             m.wait_recv()
 
-    def last(self, n, k, d):
-        l, g = self.l, self.g(n)
-        return l.copy(g.at[l.x, l.y, l.c], self.r4.at[k, d - 1], self.base + 6 * n + 5, l.zdev((l.z + d) % 4))
-
-    def add1(self, n):
-        l, g = self.l, self.g(n)
-        for a in range(2):
-            for b in range(2):
-                ref = g.at[a, b, l.c]
-                ref[...] = ref[...] + self.r1[n, a, b]
-
-    def add2(self, n):
-        l, g = self.l, self.g(n)
-        for a in range(2):
-            ref = g.at[a, l.y, l.c, 0:48]
-            ref[...] = ref[...] + self.r2[n, 0, a]
-            ref = g.at[l.x, a, l.c, 48:96]
-            ref[...] = ref[...] + self.r2[n, 1, a]
-
-    def add3(self, n):
-        l, g = self.l, self.g(n)
-        for h in range(2):
-            ref = g.at[l.x, l.y, l.c, pl.ds(48 * h, 48)]
-            ref[...] = ref[...] + self.r3[n, h]
+    def step(self, k, i, stage):
+        l, g, n = self.l, self.g(k, i), 4 * k + i
+        self.wait(k, i, stage - 1)
+        if stage == 2:
+            for a in range(2):
+                for b in range(2):
+                    ref = g.at[a, b, l.c]
+                    ref[...] = ref[...] + self.r1[n, a, b]
+        elif stage == 3:
+            for a in range(2):
+                ref = g.at[a, l.y, l.c, 0:48]
+                ref[...] = ref[...] + self.r2[n, 0, a]
+                ref = g.at[l.x, a, l.c, 48:96]
+                ref[...] = ref[...] + self.r2[n, 1, a]
+        else:
+            for h in range(2):
+                ref = g.at[l.x, l.y, l.c, pl.ds(48 * h, 48)]
+                ref[...] = ref[...] + self.r3[n, h]
+        self.start(k, i, stage)
+
+    def total(self, k):
+        l = self.l
+        fin = self.g(k, 0)[l.x, l.y, l.c].astype(F32)
+        for i in (1, 2, 3):
+            self.wait(k, i, 4)
+            fin = fin + self.r4[k, i - 1].astype(F32)
+        return fin
+
+    def drain(self):
+        for k in range(3):
+            for i in range(4):
+                for stage in (1, 2, 3, 4):
+                    for m in self.moves(k, i, stage):
+                        m.wait_send()
 
 
 class Rows:
@@ -452,7 +466,7 @@
             @pl.when(l.z == me)
             def _():
                 sent = 0
-                for slot in range(slots):
+                for slot in slots:
                     for step in range(4):
                         dev = (me + step) % 4
                         owner, idx = self.home(self.TABLE[dev, slot])
@@ -479,7 +493,7 @@
                             recv_sem=l.recv.at[base + slot], device_id=l.zdev(owner), device_id_type=MESH,
                         ).wait_recv()
 
-    def outward(self, rows, held, base, do):
+    def outward(self, rows, held, base, mine, do):
         l = self.l
         for me in range(4):
 
@@ -490,7 +504,7 @@
                     src = rows.at[pl.ds(7 * slot, 7)]
                     if owner == me:
                         if do != "drain":
-                            c = pltpu.make_async_copy(src, held.at[idx], self.local.at[base + slot])
+                            c = pltpu.make_async_copy(src, held.at[idx], self.local.at[mine + slot])
                             c.start() if do == "start" else c.wait()
                     elif do != "wait":
                         c = pltpu.make_async_remote_copy(
@@ -508,122 +522,326 @@
                             ).wait_recv()
 
 
-XS, CS, GS = 0, 13, 13 + 9
-AG0 = GS + 9
-
-
-def gather_kernel(x_in, cot_in, shard, x, cot, w, send, recv, local):
+XS, CS, BS = 0, 13, 22
+AG0 = BS + 3
+RET0 = AG0 + AG_SEMS
+DX0 = RET0 + 9
+SH0 = DX0 + 9
+VS0 = SH0 + 3
+RS0 = VS0 + 10
+SEMS = RS0 + RS_SEMS
+X_SLOTS = (0, 1, 2, 3, 4, 5, 6, 7, 9, 10, 11, 12)
+
+ORD = (0, 1, 3, 2)
+BACK = (2, 1, 3, 0)
+BLOCKS = ((0, 0), (1, 0), (0, 1), (0, 3), (0, 2), (2, 0), (1, 1), (2, 1), (1, 3), (2, 3), (1, 2), (2, 2))
+
+
+PLACES = (
+    [("M", n, j) for n in range(4) for j in range(5)] + ["N"] + [("B", n, j) for n in range(4) for j in range(3)]
+    + ["T0", "T1", "T2", "S0", "S1", "S2", "S3", "S4", "T3"]
+)
+TICKS = {1: ("F", 0, 0), 2: ("F", 0, 2), 3: ("F", 1, 1), 4: ("F", 2, 1), 5: ("F", 3, 1), 6: "L", 7: ("M", 0, 0), 8: ("M", 0, 4),
+         9: ("M", 1, 1), 10: ("M", 1, 4), 11: ("M", 2, 1)}
+MLP_LAGS = ((0, 6, 11), (1, 8, 12))
+BWD_LAGS = (0, 3, 5)
+
+
+def timetable():
+    plan = {}
+
+    def put(place, *event):
+        plan.setdefault(place, []).append(event)
+
+    for s, place in TICKS.items():
+        put(place, "tick", s)
+    for n in range(4):
+        for k, lags in zip((2, 1), MLP_LAGS):
+            made = PLACES.index(("M", n, 4)) + 1
+            for stage, lag in zip((2, 3, 4), lags):
+                put(PLACES[made + lag], "step", k, ORD[n], stage)
+        made = PLACES.index(("B", n, 2)) + 1
+        for stage, lag in zip((2, 3, 4), BWD_LAGS):
+            put(PLACES[made + lag], "step", 0, BACK[n], stage)
+    return plan
+
+
+def whole_kernel(
+    x_in, cot_in, shard, small, mask_ref, vec_ref, ktail_ref, fwd_ref, back_ref, tab_ref, tabt_ref,
+    own, out_h, dx_h, vg_out, tg_out,
+    w, r1, r2, r3, r4, x, cot, sm, ob, dx, gn, hid, gn2, gs, gsr, vg, tg, vr, tr,
+    nrm, proj, qaug, kaug, vals, probs, att, nr2, act, gup, gml, dqkv, send, recv, local,
+):
+    links = Links(send, recv)
+    z = links.z
+    rows_of = Rows(links, local)
+    ag = Gather(links, shard, w, local.at[pl.ds(40, 3)], AG0)
+    rs = Scatter(links, w, r1, r2, r3, r4, RS0)
+    g1, b1, pb, g2, b2, fb = (vec_ref[i : i + 1, :] for i in range(6))
+
+    def rank(order, m):
+        i = jnp.int32(order[3])
+        for n in range(3):
+            i = jnp.where(m == n, order[n], i)
+        return (z + 4 - i) % 4
+
+    def weight(k, t):
+        return w[k, t].reshape(768, 768)
+
+    def tick(s):
+        if s + 2 < 12:
+            ag.along(*BLOCKS[s + 2])
+        if s + 1 < 12:
+            ag.across(*BLOCKS[s + 1])
+        ag.corner(*BLOCKS[s])
+
+    def at(m, plan):
+        for n, todo in plan.items():
+
+            @pl.when(m == n)
+            def _():
+                for f in todo:
+                    f()
+
+    plan = timetable()
+
+    def run(events):
+        for what, *which in events:
+            if what == "tick":
+                tick(*which)
+            else:
+                rs.step(*which)
+
+    def now(place):
+        run(plan.get(place, ()))
+
+    def hook(m, loop, j):
+        for n in range(4):
+            todo = plan.get((loop, n, j))
+            if todo:
+
+                @pl.when(m == n)
+                def _():
+                    run(todo)
+
+    def stats(v):
+        mu = jnp.mean(v, axis=-1, keepdims=True)
+        c = v - mu
+        var = jnp.mean(c * c, axis=-1, keepdims=True)
+        return c, lax.rsqrt(var + 1e-6)
+
     x[63] = jnp.zeros((8, 768), BF)
     cot[63] = jnp.zeros((8, 768), BF)
-    links = Links(send, recv)
     links.barrier()
-    rows = Rows(links, local)
-    ag = Gather(links, shard, w, local.at[pl.ds(40, 3)], AG0)
-    rows.inward(x_in, x, 13, XS, "start")
-    ag.own(0)
-    rows.inward(cot_in, cot, 9, CS, "start")
-    order = [("along", 0), ("own", 1), ("across", 0), ("along", 1), ("own", 2), ("corner", 0), ("across", 1), ("along", 2),
-             ("corner", 1), ("across", 2), ("corner", 2)]
-    for kind, k in order:
-        if kind == "own":
-            ag.own(k)
-        else:
-            for i in (range(1, 4) if kind == "along" else range(4)):
-                getattr(ag, kind)(k, i)
-    for k in range(3):
-        ag.partner(k)
-    rows.inward(x_in, x, 13, XS, "wait")
-    rows.inward(cot_in, cot, 9, CS, "wait")
-    rows.inward(x_in, x, 13, XS, "drain")
-    rows.inward(cot_in, cot, 9, CS, "drain")
-    ag.drain()
-
-
-def gather_call(xh, coth, shard):
-    shp = jax.ShapeDtypeStruct
-    vm = pl.BlockSpec(memory_space=pltpu.VMEM)
-    n = AG0 + AG_SEMS
-    return pl.pallas_call(
-        gather_kernel,
-        out_shape=(shp((NE // 8, 8, 768), BF), shp((NR // 8, 8, 768), BF), shp((3, 4, 2, 2, 2, 96, 768), BF)),
-        in_specs=[vm] * 3,
-        out_specs=(vm,) * 3,
-        scratch_shapes=[pltpu.SemaphoreType.DMA((n,)), pltpu.SemaphoreType.DMA((n,)), pltpu.SemaphoreType.DMA((48,))],
-        compiler_params=pltpu.CompilerParams(collective_id=0, has_side_effects=True, vmem_limit_bytes=67043328),
-    )(xh, coth, shard)
-
-
-RET0 = 0
-DX0 = 9
-SH0 = 18
-VS0 = 21
-RS0 = VS0 + 10
-
-
-def scatter_kernel(g_in, x, mask_ref, gain_ref, gn_ref, gh_ref, vg_in, tg_in, out,
-                   own, out_h, dx_h, vg_out, tg_out,
-                   g, r1, r2, r3, r4, gs, gsr, dx, vg, tg, vr, tr, send, recv, local):
-    links = Links(send, recv)
-    for n in range(12):
-        pltpu.make_async_copy(g_in.at[n // 4, (links.z + n % 4 + 1) % 4], g.at[n], local.at[20 + n]).start()
-    links.barrier()
-    rows = Rows(links, local)
-    rs = Scatter(links, lambda n: g.at[n], r1, r2, r3, r4, RS0)
-    rows.outward(out, out_h, RET0, "start")
-    gs[...] = gn_ref[NR:].reshape(WR // 8, 8, 768).astype(BF)
+    for b in (0, 1):
+        ag.along(*BLOCKS[b])
+    bias = [links.copy(small, sm.at[z], BS + d - 1, links.zdev((z + d) % 4)) for d in (1, 2, 3)]
+    keep_bias = pltpu.make_async_copy(small, sm.at[z], local.at[43])
+    keep_bias.start()
+    for c in bias:
+        c.start()
+    rows_of.inward(x_in, x, X_SLOTS, XS, "start")
+    ag.own_z(0)
+    rows_of.inward(cot_in, cot, range(9), CS, "start")
+    ag.own_z(1)
+
+    vg[...] = jnp.zeros_like(vg)
+    tg[...] = jnp.zeros_like(tg)
+    rows_of.inward(x_in, x, X_SLOTS, XS, "wait")
+    x[56:63] = x[pl.ds(NR // 8 + 7 * z, 7)]
+    for c in bias:
+        c.wait_recv()
+    keep_bias.wait()
+
+    for r0 in range(0, NE, 32):
+        rows = slice(r0, r0 + 32)
+        c, rstd = stats(x[r0 // 8 : r0 // 8 + 4].astype(F32).reshape(32, 768))
+        nrm[rows, :] = (mask_ref[rows, :] * (c * rstd * g1 + b1)).astype(BF)
+
+    ag.across(*BLOCKS[0])
+    tick(0)
+    ag.own_z(2)
+    mix = gn.at[pl.ds(0, NR)]
+    mix[...] = jnp.zeros_like(mix)
+
+    def fwd_t(m, _):
+        at(m, {n: [partial(ag.partner, 0, ORD[n])] for n in range(4)})
+        t = rank(ORD, m)
+        proj[...] = dotf(nrm[...], weight(0, t)[:, :576], NN) + sm[t][1:2, :576]
+        for h in range(3):
+            hh = 3 * t + h
+            qs = (proj[:NR, 64 * h : 64 * h + 64].astype(BF) * BF(0.125)).astype(BF)
+            rel = dotf(qs, tabt_ref[...], NN)
+            lane = lax.broadcasted_iota(jnp.int32, (NR, 128), 1)
+            got = jnp.take_along_axis(rel, fwd_ref[...], axis=1, mode="promise_in_bounds")
+            hi = got.astype(BF).astype(F32)
+            tail = jnp.where(lane < 92, hi, got - hi)
+            tail = jnp.where(lane == 120, 1.0, jnp.where(lane < 120, tail, 0.0)).astype(BF)
+            qa = jnp.concatenate([qs, tail[:, 64:]], axis=1)
+            qaug[hh] = qa
+            for wn in range(3):
+                src = slice(wn * WR, wn * WR + WR) if wn < 2 else slice(NR, NE)
+                k = proj[src, 192 + 64 * h : 256 + 64 * h].astype(BF)
+                kaug[hh, wn] = jnp.concatenate([k, ktail_ref[:, 64:]], axis=1)
+                vals[hh, wn] = proj[src, 384 + 64 * h : 448 + 64 * h].astype(BF)
+        hook(m, "F", 0)
+        for h in range(3):
+            hh = 3 * t + h
+            for wn in range(3):
+                rows = slice(wn * WR, wn * WR + WR) if wn < 2 else slice(2 * WR, NR)
+                s = dotf(qaug[hh, rows, :], kaug[hh, wn], NT)
+                e = jnp.exp(s - jnp.max(s, axis=-1, keepdims=True))
+                p = (e * (1.0 / jnp.sum(e, axis=-1, keepdims=True))).astype(BF)
+                probs[hh, rows, :] = p
+                att[t, rows, 64 * h : 64 * h + 64] = dotf(p, vals[hh, wn], NN).astype(BF)
+            if h == 1:
+                hook(m, "F", 1)
+        mix[...] += dotf(att[t], weight(0, t)[:, 576:], NT)
+        hook(m, "F", 2)
+        return 0
+
+    lax.fori_loop(0, 4, fwd_t, 0)
+    rows_of.inward(cot_in, cot, range(9), CS, "wait")
+    now("L")
+
+    for r0 in range(0, NR, 32):
+        rows = slice(r0, r0 + 32)
+        xv = x[r0 // 8 : r0 // 8 + 4].astype(F32).reshape(32, 768)
+        hv = xv + mask_ref[rows, :] * (mix[rows, :] + pb)
+        hid[rows, :] = hv
+        c, rstd = stats(hv)
+        nr2[rows, :] = (c * rstd * g2 + b2).astype(BF)
+        gm = mask_ref[rows, :] * cot[r0 // 8 : r0 // 8 + 4].astype(F32).reshape(32, 768)
+        gml[rows, :] = gm.astype(BF)
+    mix[...] = jnp.zeros_like(mix)
+    gn2[...] = jnp.zeros_like(gn2)
+
+    def mlp_t(m, _):
+        at(m, {n: [partial(ag.partner, 1, ORD[n]), partial(ag.partner, 2, ORD[n])] for n in range(4)})
+        t = rank(ORD, m)
+        for f in range(3):
+            cols = slice(256 * f, 256 * f + 256)
+            for r0 in range(0, NR, 128):
+                rows = slice(r0, r0 + 128)
+                up = dotf(nr2[rows, :], weight(1, t)[:, cols], NN) + sm[t][0:1, cols]
+                ga = dotf(gml[rows, :], weight(2, t)[:, cols], NN)
+                cdf = 0.5 * (1.0 + lax.erf(up * (1.0 / math.sqrt(2.0))))
+                pdf = jnp.exp(-0.5 * up * up) * (1.0 / math.sqrt(2.0 * math.pi))
+                act[rows, cols] = (up * cdf).astype(BF)
+                gup[rows, cols] = (ga * (cdf + up * pdf)).astype(BF)
+            hook(m, "M", f)
+        vg[0, pl.ds(8 + t, 1), :] = jnp.sum(gup[...].astype(F32), axis=0, keepdims=True)
+        mix[...] += dotf(act[...], weight(2, t), NT)
+        hook(m, "M", 3)
+        gn2[...] += dotf(gup[...], weight(1, t), NT)
+        hook(m, "M", 4)
+        at(m, {n: [partial(ag.drain, 2, ORD[n])] for n in range(4)})
+        w[2, t] = dotf(gml[...], act[...], TN).astype(BF).reshape(2, 2, 2, 96, 768)
+        at(m, {n: [partial(rs.start, 2, ORD[n], 1), partial(ag.drain, 1, ORD[n])] for n in range(4)})
+        w[1, t] = dotf(nr2[...], gup[...], TN).astype(BF).reshape(2, 2, 2, 96, 768)
+        at(m, {n: [partial(rs.start, 1, ORD[n], 1)] for n in range(4)})
+        return 0
+
+    lax.fori_loop(0, 4, mlp_t, 0)
+    now("N")
+
+    sums = [jnp.zeros((8, 768), F32) for _ in range(4)]
+
+    def fold(v):
+        return jnp.sum(v.reshape(4, 8, 768), axis=0)
+
+    gbl = act
+    for r0 in range(0, NR, 32):
+        rows = slice(r0, r0 + 32)
+        mk = mask_ref[rows, :]
+        gm = mk * cot[r0 // 8 : r0 // 8 + 4].astype(F32).reshape(32, 768)
+        hv = hid[rows, :]
+        ob[r0 // 8 : r0 // 8 + 4] = (mk * (hv + mix[rows, :] + fb)).reshape(4, 8, 768).astype(BF)
+        c, rstd = stats(hv)
+        xh = c * rstd
+        gv = gn2[rows, :]
+        e2 = gv * g2
+        gh = gm + rstd * (e2 - jnp.mean(e2, axis=-1, keepdims=True) - xh * jnp.mean(e2 * xh, axis=-1, keepdims=True))
+        gb = mk * gh
+        hid[rows, :] = gh
+        gbl[rows, :] = gb.astype(BF)
+        for n, v in enumerate((gv * xh, gv, gb, gm)):
+            sums[n] = sums[n] + fold(v)
+    for n in range(4):
+        vg[0, n : n + 1, :] = jnp.sum(sums[n], axis=0, keepdims=True)
+    rows_of.outward(ob, out_h, RET0, 22, "start")
+    gn[...] = jnp.zeros_like(gn)
+
+    def bwd_t(m, _):
+        t = rank(BACK, m)
+        at(m, {n: [partial(ag.drain, 0, BACK[n])] for n in range(4)})
+        att_w = att[t]
+        proj[:NR, :192] = dotf(gbl[...], weight(0, t)[:, 576:], NN)
+        dqkv[...] = jnp.zeros_like(dqkv)
+        for h in range(3):
+            hh = 3 * t + h
+            lo = 64 * h
+            for wn in range(3):
+                rows = slice(wn * WR, wn * WR + WR) if wn < 2 else slice(2 * WR, NR)
+                dst = rows if wn < 2 else slice(NR, NE)
+                do = proj[rows, lo : lo + 64].astype(BF)
+                p = probs[hh, rows, :]
+                pf = p.astype(F32)
+                dp = dotf(do, vals[hh, wn], NT)
+                delta = jnp.sum(pf * dp, axis=-1, keepdims=True)
+                ds = (pf * (dp - delta)).astype(BF)
+                dq = dotf(ds, kaug[hh, wn], NN)
+                qa = qaug[hh, rows, :]
+                dqkv[dst, 192 + lo : 256 + lo] = dotf(ds, qa, TN)[:, :64].astype(BF)
+                dqkv[dst, 384 + lo : 448 + lo] = dotf(p, do, TN).astype(BF)
+                rel = jnp.take_along_axis(dq, back_ref[rows, :], axis=1, mode="promise_in_bounds").astype(BF)
+                gq = dq[:, :64] * 0.125 + dotf(rel, tab_ref[...], NN)
+                dqkv[rows, lo : lo + 64] = gq.astype(BF)
+                tg[0] += dotf(rel, qa, TN)[:64]
+            hook(m, "B", h)
+        vg[0, pl.ds(12 + t, 1), 0:576] = jnp.sum(dqkv[...].astype(F32), axis=0, keepdims=True)
+        gn[...] += dotf(dqkv[...], weight(0, t)[:, :576], NT)
+        gw = jnp.concatenate([dotf(nrm[...], dqkv[...], TN).astype(BF), dotf(gbl[...], att_w, TN).astype(BF)], axis=1)
+        w[0, t] = gw.reshape(2, 2, 2, 96, 768)
+        at(m, {n: [partial(rs.start, 0, BACK[n], 1)] for n in range(4)})
+        return 0
+
+    lax.fori_loop(0, 4, bwd_t, 0)
+
+    gs[...] = gn[NR:].reshape(WR // 8, 8, 768).astype(BF)
     sh = [
-        links.copy(gs.at[pl.ds(7 * ((links.z + d) % 4), 7)], gsr.at[d - 1], SH0 + d - 1, links.zdev((links.z + d) % 4))
-        for d in (1, 2, 3)
+        links.copy(gs.at[pl.ds(7 * ((z + d) % 4), 7)], gsr.at[d - 1], SH0 + d - 1, links.zdev((z + d) % 4)) for d in (1, 2, 3)
     ]
     for c in sh:
         c.start()
-
-    for n in range(12):
-        pltpu.make_async_copy(g_in.at[n // 4, (links.z + n % 4 + 1) % 4], g.at[n], local.at[20 + n]).wait()
-        rs.start(n, 1)
+    now("T0")
     for c in sh:
         c.wait_recv()
-    first_norm_back(links, x, mask_ref, gain_ref, gn_ref, gh_ref, gs, gsr, dx, vg_in, vg.at[0])
-    rows.outward(dx, dx_h, DX0, "start")
-    tg[0] = tg_in[...]
-    for n in range(12):
-        rs.wait(n, 1)
-        rs.add1(n)
-        rs.start(n, 2)
-    for n in range(12):
-        rs.wait(n, 2)
-        rs.add2(n)
-        rs.start(n, 3)
-    for n in range(12):
-        rs.wait(n, 3)
-        rs.add3(n)
-        if n % 4 < 3:
-            rs.last(n, n // 4, n % 4 + 1).start()
-    small_sums(links, vg, tg, vr, tr)
+    now("T1")
+    first_norm_back(links, x, mask_ref, vec_ref, gn, hid, gsr, dx, vg.at[0])
+    rows_of.outward(dx, dx_h, DX0, 31, "start")
+    now("T2")
+    small_sums(links, vg, tg, vr, tr, now)
+    now("T3")
     vg_out[...] = vg[5]
     tg_out[...] = tg[5]
+    for k in (2, 1, 0):
+        own[k] = rs.total(k)
+    rows_of.outward(ob, out_h, RET0, 22, "wait")
+    rows_of.outward(dx, dx_h, DX0, 31, "wait")
+    rows_of.outward(ob, out_h, RET0, 22, "drain")
+    rows_of.outward(dx, dx_h, DX0, 31, "drain")
+    rows_of.inward(x_in, x, X_SLOTS, XS, "drain")
+    rows_of.inward(cot_in, cot, range(9), CS, "drain")
+    for c in sh + bias:
+        c.wait_send()
     for k in range(3):
-        for d in (1, 2, 3):
-            rs.last(4 * k + d - 1, k, d).wait_recv()
-        fin = g[4 * k + 3, links.x, links.y, links.c].astype(F32)
-        for d in range(3):
-            fin = fin + r4[k, d].astype(F32)
-        own[k] = fin
-    rows.outward(out, out_h, RET0, "wait")
-    rows.outward(dx, dx_h, DX0, "wait")
-    rows.outward(out, out_h, RET0, "drain")
-    rows.outward(dx, dx_h, DX0, "drain")
-    for c in sh:
-        c.wait_send()
-    for n in range(12):
-        for stage in (1, 2, 3):
-            for m in rs.moves(n, stage):
-                m.wait_send()
-        if n % 4 < 3:
-            rs.last(n, n // 4, n % 4 + 1).wait_send()
-
-
-def first_norm_back(links, x, mask_ref, gain_ref, gn_ref, gh_ref, gs, gsr, dx, vg_in, vg):
+        for i in (1, 2, 3):
+            ag.move(k, "z", i).wait_send()
+    rs.drain()
+
+
+def first_norm_back(links, x, mask_ref, gain_ref, gn_ref, gh_ref, gsr, dx, vg):
     own = gn_ref[pl.ds(pl.multiple_of(NR + 56 * links.z, 8), 56), :]
     for d in range(3):
         own = own + gsr[d].astype(F32).reshape(56, 768)
@@ -645,12 +863,11 @@
         dx[r0 // 8 : (r0 + n) // 8] = gx.reshape(n // 8, 8, 768).astype(BF)
         s_gain = s_gain + jnp.sum((gn * xh).reshape(n // 8, 8, 768), axis=0)
         s_bias = s_bias + jnp.sum(gn.reshape(n // 8, 8, 768), axis=0)
-    vg[...] = vg_in[...]
     vg[4:5, :] = jnp.sum(s_gain, axis=0, keepdims=True)
     vg[5:6, :] = jnp.sum(s_bias, axis=0, keepdims=True)
 
 
-def small_sums(links, vg, tg, vr, tr):
+def small_sums(links, vg, tg, vr, tr, now):
     l = links
     partners = [l.sib, l.xn, l.yn, l.zdev((l.z // 2) * 2 + 1 - l.z % 2), l.zdev((l.z + 2) % 4)]
     copies = []
@@ -658,6 +875,7 @@
         pair = [l.copy(vg.at[n], vr.at[n], VS0 + 2 * n, dev), l.copy(tg.at[n], tr.at[n], VS0 + 2 * n + 1, dev)]
         for c in pair:
             c.start()
+        now(f"S{n}")
         for c in pair:
             c.wait_recv()
         vg[n + 1] = vg[n] + vr[n]
@@ -667,26 +885,31 @@
         c.wait_send()
 
 
-def scatter_call(grads, x, mask, vec, gn, gh, vg, tg, out):
+def whole_call(xh, coth, shard, small, mask, vec, ktail, fwd, back, tab, tabt):
     shp = jax.ShapeDtypeStruct
     vm = pl.BlockSpec(memory_space=pltpu.VMEM)
-    n = RS0 + RS_SEMS
+    hbm = pl.BlockSpec(memory_space=pl.ANY)
+    V = pltpu.VMEM
+    dma = pltpu.SemaphoreType.DMA
     return pl.pallas_call(
-        scatter_kernel,
+        whole_kernel,
         out_shape=(
             shp((3, 96, 768), F32), shp((9, 7, 8, 768), BF), shp((9, 7, 8, 768), BF), shp((16, 768), F32), shp((64, 128), F32),
         ),
-        in_specs=[pl.BlockSpec(memory_space=pl.ANY)] + [vm] * 8,
-        out_specs=(vm,) * 5,
+        in_specs=[hbm, hbm] + [vm] * 9,
+        out_specs=(vm, hbm, hbm, vm, vm),
         scratch_shapes=[
-            pltpu.VMEM((12, 2, 2, 2, 96, 768), BF), pltpu.VMEM((12, 2, 2, 96, 768), BF), pltpu.VMEM((12, 2, 2, 48, 768), BF),
-            pltpu.VMEM((12, 2, 48, 768), BF), pltpu.VMEM((3, 3, 96, 768), BF), pltpu.VMEM((WR // 8, 8, 768), BF),
-            pltpu.VMEM((3, 7, 8, 768), BF), pltpu.VMEM((NR // 8, 8, 768), BF), pltpu.VMEM((6, 16, 768), F32),
-            pltpu.VMEM((6, 64, 128), F32), pltpu.VMEM((5, 16, 768), F32), pltpu.VMEM((5, 64, 128), F32),
-            pltpu.SemaphoreType.DMA((n,)), pltpu.SemaphoreType.DMA((n,)), pltpu.SemaphoreType.DMA((32,)),
+            V((3, 4, 2, 2, 2, 96, 768), BF), V((12, 2, 2, 96, 768), BF), V((12, 2, 2, 48, 768), BF), V((12, 2, 48, 768), BF),
+            V((3, 3, 96, 768), BF), V((NE // 8, 8, 768), BF), V((NR // 8, 8, 768), BF), V((4, 8, 768), F32),
+            V((NR // 8, 8, 768), BF), V((NR // 8, 8, 768), BF), V((NE, 768), F32), V((NR, 768), F32), V((NR, 768), F32),
+            V((WR // 8, 8, 768), BF), V((3, 7, 8, 768), BF), V((6, 16, 768), F32), V((6, 64, 128), F32),
+            V((5, 16, 768), F32), V((5, 64, 128), F32),
+            V((NE, 768), BF), V((NE, 576), F32), V((HEADS, NR, 128), BF), V((HEADS, 3, WR, 128), BF), V((HEADS, 3, WR, 64), BF),
+            V((HEADS, NR, WR), BF), V((4, NR, 192), BF), V((NR, 768), BF), V((NR, 768), BF), V((NR, 768), BF), V((NR, 768), BF),
+            V((NE, 576), BF), dma((SEMS,)), dma((SEMS,)), dma((48,)),
         ],
-        compiler_params=pltpu.CompilerParams(collective_id=1, has_side_effects=True, vmem_limit_bytes=67043328),
-    )(grads, x, mask, vec, gn, gh, vg, tg, out)
+        compiler_params=pltpu.CompilerParams(collective_id=0, has_side_effects=True, vmem_limit_bytes=67043328),
+    )(xh, coth, shard, small, mask, vec, ktail, fwd, back, tab, tabt)
 
 
 def plain_gather(xh, coth, shard):
@@ -739,8 +962,7 @@
             fc2_weight.T,
         ]
     )
-    x, cot, whole = (gather_call if links else plain_gather)(home_blocks(tokens), home_blocks(out_grad), shard)
-    whole = whole.reshape(3, 4, 768, 768)
+    xh, coth = home_blocks(tokens), home_blocks(out_grad)
 
     wi, wj, wv = token_positions()
     wi, wj, wv = jnp.asarray(wi, jnp.int32), jnp.asarray(wj, jnp.int32), jnp.asarray(wv)
@@ -763,12 +985,8 @@
     jj = jnp.concatenate([wj, wj, qj])
     fwd, back = pick_lanes(ii, jj)
 
-    small = jnp.concatenate(
-        [fc1_bias[None], jnp.pad(qv_bias.reshape(1, 384), ((0, 0), (0, 384))), jnp.zeros((14, 768), BF)], axis=0
-    )
-    small = lax.all_gather(small, "tensor", axis=0).astype(F32)
-    fc1b = small[:, 0:1, :]
-    qkvb = jnp.concatenate([small[:, 1:2, :192], jnp.zeros((4, 1, 192), F32), small[:, 1:2, 192:384]], axis=2)
+    small = jnp.zeros((8, 768), F32).at[0].set(fc1_bias.astype(F32))
+    small = small.at[1, :192].set(qv_bias[0].astype(F32)).at[1, 384:576].set(qv_bias[1].astype(F32))
     vec = jnp.stack(
         [norm1_gain, norm1_bias, proj_bias, norm2_gain, norm2_bias, fc2_bias, fc2_bias, fc2_bias]
     ).astype(F32)
@@ -776,10 +994,15 @@
     tabt = (tab * BF(8)).T
     ktail = jnp.asarray(key_tail(), BF)
 
-    out, gn, gh, grads, vg, tg = compute(x, cot, mask, whole, vec, qkvb, fc1b, ktail, fwd, back, tab, tabt)
-    own, out, dx, vg, tg = (scatter_call if links else plain_scatter)(
-        grads.reshape(3, 4, 2, 2, 2, 96, 768), x, mask[:NR], vec, gn, gh, vg, tg, out
-    )
+    if links:
+        own, out, dx, vg, tg = whole_call(xh, coth, shard, small, mask, vec, ktail, fwd, back, tab, tabt)
+    else:
+        x, cot, whole = plain_gather(xh, coth, shard)
+        small = lax.all_gather(small, "tensor", axis=0)
+        out, gn, gh, grads, vg, tg = compute(
+            x, cot, mask, whole.reshape(3, 4, 768, 768), vec, small[:, 1:2, :576], small[:, 0:1], ktail, fwd, back, tab, tabt
+        )
+        own, out, dx, vg, tg = plain_scatter(grads, x, mask[:NR], vec, gn, gh, vg, tg, out)
 
     def tokens_of(blocks):
         return blocks.reshape(9, BP, 768)[:, :BT].reshape(tokens.shape)

time: 338 us -> 238 us (0.70)
  Pallas kernels: 276 us -> 189 us
  blocking collectives: 13.4 us -> 0 us
    pallas_call x3 -> x1, Pallas kernels: 276 us -> 189 us  [whole_call(): pl.pallas_call(whole_kernel, out_shape=(shp((3, 96, 768), F32), shp((9, 7...]
    all_gather x1 -> x0, blocking collectives: 13.4 us -> none  [per_device(): small = lax.all_gather(small, 'tensor', axis=0).astype(F32)]
where the time goes in v2:
time: 238 us; the launch traced here: 237 us
  Pallas kernels  189 us (79%)
  local copies, waits for them, and re-layouts  27.6 us (12%)
  between operations  11.4 us (5%)
  other arithmetic  9.04 us (4%)
    pallas_call x1, Pallas kernels, whole_call(): pl.pallas_call(whole_kernel, out_shape=(shp((3, 96, 768), F32), shp((9, 7...  189 us
    unnamed x40, local copies, waits for them, and re-layouts  5.27 us

profile of v2, /device:TPU:0, one launch (start us, length us, event | category | flops | bytes accessed | tf_op | source)
XLA Modules:
  0.0 237.4 jit_solution(2917028989674061696)
XLA Ops:
  0.7 0.8 dynamic_slice.15
  1.5 0.8 dynamic_slice.16
  2.2 0.7 dynamic_slice.14
  4.4 0.8 slice_convert_fusion.1
  22.6 0.7 compare_and_fusion.2
  23.4 0.9 pad_add_fusion
  24.9 0.8 copy.81
  25.7 0.8 copy.82
  27.4 0.7 copy.84.tab_ref
  28.7 0.9 copy.79
  29.6 1.1 copy.78
  30.9 0.8 pad_maximum_fusion.shard
  31.7 0.9 copy.83.mask_ref
  32.7 1.1 add_select_fusion
  34.2 1.3 pad_bitcast_fusion
  35.4 189.3 %shard_map.414 = (f32[3,96,768]{2,1,0:T(8,128)}, bf16[9,7,8,768]{3,2,1,0:T(8,128)(2,1)}, bf16[9,7,8,768]{3,2,1,0:T(8,128)(2,1)}, f32[16,768]{1,0:T(8,128)}, f32[64,128]{1,0:T(8,128)}) custom-call(bf16[9,7,8,768]{3,2,1,0:T(8,128)(2,1)} %get-tuple-element.177.x_in, bf16[9,7,8,768]{3,2,1,0:T(8,128)(2,1)} %get-tuple-element.176.cot_in, ...), custom_call_target="tpu_custom_call" | custom-call | tf_op jit(solution)/shard_map/pallas_call | solution.py:894
  224.8 2.2 reshape.365
  227.0 0.7 fusion.8
  228.5 0.7 slice.174
  229.3 1.6 slice_reduce_fusion
  232.2 0.7 copy.87
  233.0 0.8 slice_bitcast_fusion
  234.0 0.9 copy.86
  235.0 2.5 %reshape.368 = f32[1,3,147,768]{3,0,2,1:T(1,128)} reshape(f32[9,49,768]{2,1,0:T(8,128)S(1)} %slice_convert_fusion) | data formatting | bytes 2709504 | tf_op jit(solution)/shard_map/convert_element_type | solution.py:1011
  (76 shorter events, 13.4 us)
Async XLA Ops:
  0.6 30.3 %copy-start.4 = (bf16[768,96]{0,1:T(8,128)(2,1)S(1)}, bf16[768,96]{0,1:T(8,128)(2,1)}, u32[]{:S(2)}) copy-start(bf16[768,96]{0,1:T(8,128)(2,1)} %param.55) | copy-start | bytes 442372
  0.7 30.3 %copy-start.5 = (bf16[96,768]{1,0:T(8,128)(2,1)S(1)}, bf16[96,768]{1,0:T(8,128)(2,1)}, u32[]{:S(2)}) copy-start(bf16[96,768]{1,0:T(8,128)(2,1)} %param.53) | copy-start | bytes 442372
  10.1 22.6 %copy-start.8 = (s32[128]{0:T(128)S(1)}, s32[128]{0:T(128)}, u32[]{:S(2)}) copy-start(s32[128]{0:T(128)} %constant.309) | copy-start | bytes 1540
  10.1 22.6 %copy-start.9 = (s32[128]{0:T(128)S(1)}, s32[128]{0:T(128)}, u32[]{:S(2)}) copy-start(s32[128]{0:T(128)} %constant.308) | copy-start | bytes 1540
  10.1 22.6 %copy-start.10 = (s32[128]{0:T(128)S(1)}, s32[128]{0:T(128)}, u32[]{:S(2)}) copy-start(s32[128]{0:T(128)} %constant.307) | copy-start | bytes 1540
  10.1 22.6 %copy-start.11 = (s32[128]{0:T(128)S(1)}, s32[128]{0:T(128)}, u32[]{:S(2)}) copy-start(s32[128]{0:T(128)} %constant.306) | copy-start | bytes 1540
  10.1 22.6 %copy-start.12 = (pred[128]{0:T(512)(128)(4,1)S(1)}, pred[128]{0:T(512)(128)(4,1)}, u32[]{:S(2)}) copy-start(pred[128]{0:T(512)(128)(4,1)} %constant.304) | copy-start | bytes 388
  10.1 22.6 %copy-start.13 = (pred[128]{0:T(512)(128)(4,1)S(1)}, pred[128]{0:T(512)(128)(4,1)}, u32[]{:S(2)}) copy-start(pred[128]{0:T(512)(128)(4,1)} %constant.303) | copy-start | bytes 388
  10.1 22.6 %copy-start.14 = (pred[128]{0:T(512)(128)(4,1)S(1)}, pred[128]{0:T(512)(128)(4,1)}, u32[]{:S(2)}) copy-start(pred[128]{0:T(512)(128)(4,1)} %constant.301) | copy-start | bytes 388
  10.2 22.6 %copy-start.15 = (pred[128]{0:T(512)(128)(4,1)S(1)}, pred[128]{0:T(512)(128)(4,1)}, u32[]{:S(2)}) copy-start(pred[128]{0:T(512)(128)(4,1)} %constant.298) | copy-start | bytes 388
  10.2 22.6 %copy-start.16 = (pred[128]{0:T(512)(128)(4,1)S(1)}, pred[128]{0:T(512)(128)(4,1)}, u32[]{:S(2)}) copy-start(pred[128]{0:T(512)(128)(4,1)} %constant.297) | copy-start | bytes 388
  23.3 10.5 %copy-start.2 = (bf16[1,3,147,768]{3,2,1,0:T(8,128)(2,1)S(1)}, bf16[1,3,147,768]{3,2,1,0:T(8,128)(2,1)}, u32[]{:S(2)}) copy-start(bf16[1,3,147,768]{3,2,1,0:T(8,128)(2,1)} %param.41) | copy-start | bytes 2032132
  28.7 5.1 %copy-start.6 = (f32[8,768]{1,0:T(8,128)}, f32[8,768]{1,0:T(8,128)S(1)}, u32[]{:S(2)}) copy-start(f32[8,768]{1,0:T(8,128)S(1)} %scatter.30.small) | copy-start | bytes 73732
  30.9 3.0 %copy-start.3 = (bf16[1,3,147,768]{3,2,1,0:T(8,128)(2,1)S(1)}, bf16[1,3,147,768]{3,2,1,0:T(8,128)(2,1)}, u32[]{:S(2)}) copy-start(bf16[1,3,147,768]{3,2,1,0:T(8,128)(2,1)} %param.57) | copy-start | bytes 2032132
  224.8 6.7 %copy-start.7 = (f32[64,128]{1,0:T(8,128)S(1)}, f32[64,128]{1,0:T(8,128)}, u32[]{:S(2)}) copy-start(f32[64,128]{1,0:T(8,128)} %get-tuple-element.85) | copy-start | bytes 98308
  224.8 7.3 %copy-start = (f32[3,96,768]{2,1,0:T(8,128)S(1)}, f32[3,96,768]{2,1,0:T(8,128)}, u32[]{:S(2)}) copy-start(f32[3,96,768]{2,1,0:T(8,128)} %get-tuple-element.84) | copy-start | bytes 2654212
  232.2 2.7 %copy-start.1 = (bf16[9,7,8,768]{3,2,1,0:T(8,128)(2,1)S(1)}, bf16[9,7,8,768]{3,2,1,0:T(8,128)(2,1)}, u32[]{:S(2)}) copy-start(bf16[9,7,8,768]{3,2,1,0:T(8,128)(2,1)} %get-tuple-element.82) | copy-start | bytes 2322436

commit v3 on v2

--- a/solution.py
+++ b/solution.py
@@ -296,8 +296,8 @@
 
 
 class Gather:
-    def __init__(self, links, shard, w, local, base):
-        self.l, self.shard, self.w, self.local, self.base = links, shard, w, local, base
+    def __init__(self, links, shards, w, local, base):
+        self.l, self.shards, self.w, self.local, self.base = links, shards, w, local, base
 
     def sem(self, k, kind, i):
         start = {"z": 0, "x": 3, "y": 7, "hx": 11, "hy": 15, "so": 19, "sx": 23, "sy": 27, "sa": 31, "sb": 35}[kind]
@@ -313,7 +313,7 @@
     def move(self, k, kind, i):
         l = self.l
         if kind == "z":
-            src = self.shard.at[k]
+            src = self.shards[k]
             return l.copy(src, self.piece(k, 0, l.x, l.y, l.c), self.sem(k, kind, i - 1), l.zdev((l.z + i) % 4))
         px, py, half, dev = {
             "x": (l.x, l.y, None, l.xn), "y": (l.x, l.y, None, l.yn),
@@ -323,7 +323,7 @@
         }[kind]
         dst = self.piece(k, i, px, py, l.c, half)
         own = kind in ("x", "y", "so") and i == 0
-        return l.copy(self.shard.at[k] if own else dst, dst, self.sem(k, kind, i), dev)
+        return l.copy(self.shards[k] if own else dst, dst, self.sem(k, kind, i), dev)
 
     def start(self, k, kind, i):
         self.move(k, kind, i).start()
@@ -333,7 +333,7 @@
 
     def keep(self, k):
         l = self.l
-        return pltpu.make_async_copy(self.shard.at[k], self.piece(k, 0, l.x, l.y, l.c), self.local.at[k])
+        return pltpu.make_async_copy(self.shards[k], self.piece(k, 0, l.x, l.y, l.c), self.local.at[k])
 
     def own_z(self, k):
         for i in (1, 3, 2):
@@ -566,16 +566,70 @@
     return plan
 
 
+def places(rows, first):
+    r = lax.broadcasted_iota(jnp.int32, (rows, 128), 0)
+    blk = sum((r >= BP * n).astype(jnp.int32) for n in range(1, 4)) if rows == WR else jnp.zeros_like(r)
+    off = r - BP * blk
+    token = (blk + first) * BT + jnp.minimum(off, BT - 1)
+    i = (token * 4682) >> 16
+    return i, token - WS * i, off < BT
+
+
+def lanes_of(i, j):
+    lane = lax.broadcasted_iota(jnp.int32, i.shape, 1)
+    m = lane - 64
+    m = m - 28 * ((m >= 28).astype(jnp.int32) + (m >= 56).astype(jnp.int32))
+    fwd = jnp.where(m >= 14, 32 + j - (m - 14) + 13, i - m + 13)
+    fwd = jnp.where((lane >= 64) & (lane < 120), fwd, 0)
+    d = lane & 31
+    pos = jnp.where(lane >= 32, j, i) + 13 - d
+    ok = (pos >= 0) & (pos < WS) & (lane < 64) & (d < 27)
+    return fwd, jnp.where(ok, pos + jnp.where(lane >= 32, 78, 64), 127)
+
+
+def fill_tables(z, ids, mask_ref, fwd_ref, back_ref):
+    across = (GRID + WS - 1) // WS
+
+    def valid(w, i, j, ok):
+        a = lax.div(w, jnp.int32(across))
+        hi = jnp.where(w < across * across, GRID - a * WS, 0)
+        wi = GRID - (w - across * a) * WS
+        return jnp.where(ok & (i < hi) & (j < wi), 1.0, 0.0)[:, :1]
+
+    def window(n):
+        m, s = (jnp.int32(v) for v in WINDOWS_OF[3][n])
+        for dev in range(3):
+            m = jnp.where(z == dev, WINDOWS_OF[dev][n][0], m)
+            s = jnp.where(z == dev, WINDOWS_OF[dev][n][1], s)
+        return ids[m, 0, s]
+
+    i, j, ok = places(WR, 0)
+    fwd, back = lanes_of(i, j)
+    shared = ids[SHARED[0], 0, SHARED[1]]
+    for n in range(2):
+        rows = slice(n * WR, n * WR + WR)
+        fwd_ref[rows, :] = fwd
+        back_ref[rows, :] = back
+        mask_ref[rows, :] = valid(window(n), i, j, ok)
+    mask_ref[NR:NE, :] = valid(shared, i, j, ok)
+    i, j, ok = places(QR, z)
+    fwd, back = lanes_of(i, j)
+    fwd_ref[2 * WR : NR, :] = fwd
+    back_ref[2 * WR : NR, :] = back
+    mask_ref[2 * WR : NR, :] = valid(shared, i, j, ok)
+
+
 def whole_kernel(
-    x_in, cot_in, shard, small, mask_ref, vec_ref, ktail_ref, fwd_ref, back_ref, tab_ref, tabt_ref,
-    own, out_h, dx_h, vg_out, tg_out,
+    x_in, cot_in, ids, qkv_w, proj_w, fc1_w, fc2_w, vec_ref, ktail_ref, tab_ref,
+    g_qkv, g_proj, g_fc1, g_fc2, out_h, dx_h, v0, v1, v2, v3, v4, v5, fc1b_out, qvb_out, relh_out, relw_out,
+    shard0, small, mask_ref, fwd_ref, back_ref,
     w, r1, r2, r3, r4, x, cot, sm, ob, dx, gn, hid, gn2, gs, gsr, vg, tg, vr, tr,
     nrm, proj, qaug, kaug, vals, probs, att, nr2, act, gup, gml, dqkv, send, recv, local,
 ):
     links = Links(send, recv)
     z = links.z
     rows_of = Rows(links, local)
-    ag = Gather(links, shard, w, local.at[pl.ds(40, 3)], AG0)
+    ag = Gather(links, (shard0, fc1_w, fc2_w), w, local.at[pl.ds(40, 3)], AG0)
     rs = Scatter(links, w, r1, r2, r3, r4, RS0)
     g1, b1, pb, g2, b2, fb = (vec_ref[i : i + 1, :] for i in range(6))
 
@@ -630,6 +684,13 @@
         var = jnp.mean(c * c, axis=-1, keepdims=True)
         return c, lax.rsqrt(var + 1e-6)
 
+    for t in range(3):
+        shard0[:, 192 * t : 192 * t + 192] = qkv_w[t]
+    shard0[:, 576:] = proj_w[...].astype(F32).T.astype(BF)
+    small[...] = jnp.zeros_like(small)
+    small[0:1, :] = vec_ref[6:7, :]
+    small[1:2, 0:192] = vec_ref[8:9, 0:192]
+    small[1:2, 384:576] = vec_ref[9:10, 0:192]
     x[63] = jnp.zeros((8, 768), BF)
     cot[63] = jnp.zeros((8, 768), BF)
     links.barrier()
@@ -647,6 +708,7 @@
 
     vg[...] = jnp.zeros_like(vg)
     tg[...] = jnp.zeros_like(tg)
+    fill_tables(z, ids, mask_ref, fwd_ref, back_ref)
     rows_of.inward(x_in, x, X_SLOTS, XS, "wait")
     x[56:63] = x[pl.ds(NR // 8 + 7 * z, 7)]
     for c in bias:
@@ -671,7 +733,7 @@
         for h in range(3):
             hh = 3 * t + h
             qs = (proj[:NR, 64 * h : 64 * h + 64].astype(BF) * BF(0.125)).astype(BF)
-            rel = dotf(qs, tabt_ref[...], NN)
+            rel = dotf(qs, tab_ref[...], NT) * 8.0
             lane = lax.broadcasted_iota(jnp.int32, (NR, 128), 1)
             got = jnp.take_along_axis(rel, fwd_ref[...], axis=1, mode="promise_in_bounds")
             hi = got.astype(BF).astype(F32)
@@ -823,10 +885,22 @@
     now("T2")
     small_sums(links, vg, tg, vr, tr, now)
     now("T3")
-    vg_out[...] = vg[5]
-    tg_out[...] = tg[5]
-    for k in (2, 1, 0):
-        own[k] = rs.total(k)
+    for n, ref in enumerate((v0, v1, v2, v3, v4, v5)):
+        for c in range(6):
+            ref[c : c + 1, :] = vg[5, n : n + 1, 128 * c : 128 * c + 128]
+    for t in range(4):
+        for c in range(6):
+            fc1b_out[6 * t + c : 6 * t + c + 1, :] = vg[5, 8 + t : 9 + t, 128 * c : 128 * c + 128]
+        qvb_out[0:1, 192 * t : 192 * t + 192] = vg[5, 12 + t : 13 + t, 0:192]
+        qvb_out[1:2, 192 * t : 192 * t + 192] = vg[5, 12 + t : 13 + t, 384:576]
+    relh_out[...] = tg[5, 0:27, :64] * 8.0
+    relw_out[...] = tg[5, 32:59, :64] * 8.0
+    g_fc2[...] = rs.total(2)
+    g_fc1[...] = rs.total(1)
+    fin = rs.total(0)
+    for t in range(3):
+        g_qkv[t] = fin[:, 192 * t : 192 * t + 192]
+    g_proj[...] = fin[:, 576:].T
     rows_of.outward(ob, out_h, RET0, 22, "wait")
     rows_of.outward(dx, dx_h, DX0, 31, "wait")
     rows_of.outward(ob, out_h, RET0, 22, "drain")
@@ -885,7 +959,7 @@
         c.wait_send()
 
 
-def whole_call(xh, coth, shard, small, mask, vec, ktail, fwd, back, tab, tabt):
+def whole_call(xh, coth, ids, qkv_w, proj_w, fc1_w, fc2_w, vec, ktail, tab):
     shp = jax.ShapeDtypeStruct
     vm = pl.BlockSpec(memory_space=pltpu.VMEM)
     hbm = pl.BlockSpec(memory_space=pl.ANY)
@@ -894,11 +968,14 @@
     return pl.pallas_call(
         whole_kernel,
         out_shape=(
-            shp((3, 96, 768), F32), shp((9, 7, 8, 768), BF), shp((9, 7, 8, 768), BF), shp((16, 768), F32), shp((64, 128), F32),
+            shp((3, 96, 192), F32), shp((192, 96), F32), shp((96, 768), F32), shp((96, 768), F32),
+            shp((9, 7, 8, 768), BF), shp((9, 7, 8, 768), BF), *[shp((6, 128), F32)] * 6, shp((24, 128), F32),
+            shp((2, 768), F32), shp((27, 64), F32), shp((27, 64), F32),
         ),
-        in_specs=[hbm, hbm] + [vm] * 9,
-        out_specs=(vm, hbm, hbm, vm, vm),
+        in_specs=[hbm, hbm, pl.BlockSpec(memory_space=pltpu.SMEM)] + [vm] * 7,
+        out_specs=(vm, vm, vm, vm, hbm, hbm) + (vm,) * 10,
         scratch_shapes=[
+            V((96, 768), BF), V((8, 768), F32), V((NE, 1), F32), V((NR, 128), jnp.int32), V((NR, 128), jnp.int32),
             V((3, 4, 2, 2, 2, 96, 768), BF), V((12, 2, 2, 96, 768), BF), V((12, 2, 2, 48, 768), BF), V((12, 2, 48, 768), BF),
             V((3, 3, 96, 768), BF), V((NE // 8, 8, 768), BF), V((NR // 8, 8, 768), BF), V((4, 8, 768), F32),
             V((NR // 8, 8, 768), BF), V((NR // 8, 8, 768), BF), V((NE, 768), F32), V((NR, 768), F32), V((NR, 768), F32),
@@ -909,7 +986,7 @@
             V((NE, 576), BF), dma((SEMS,)), dma((SEMS,)), dma((48,)),
         ],
         compiler_params=pltpu.CompilerParams(collective_id=0, has_side_effects=True, vmem_limit_bytes=67043328),
-    )(xh, coth, shard, small, mask, vec, ktail, fwd, back, tab, tabt)
+    )(xh, coth, ids, qkv_w, proj_w, fc1_w, fc2_w, vec, ktail, tab)
 
 
 def plain_gather(xh, coth, shard):
@@ -955,6 +1032,30 @@
     def home_blocks(rows):
         return jnp.pad(rows.reshape(9, BT, 768), ((0, 0), (0, BP - BT), (0, 0))).reshape(9, 7, 8, 768)
 
+    if links:
+        vectors = (norm1_gain, norm1_bias, proj_bias, norm2_gain, norm2_bias, fc2_bias, fc1_bias)
+        row = lax.broadcasted_iota(jnp.int32, (16, 768), 0)
+        vec = jnp.pad(qv_bias.astype(F32), ((8, 6), (0, 576)))
+        for n, v in enumerate(vectors):
+            vec = jnp.where(row == n, v.astype(F32)[None, :], vec)
+        tab = jnp.pad(rel_height, ((0, 101), (0, 0))) + jnp.pad(rel_width, ((32, 69), (0, 0)))
+
+        def padded(rows):
+            return jnp.pad(rows.reshape(9, BT, 768), ((0, 0), (0, BP - BT), (0, 0))).reshape(9, 7, 8, 768)
+
+        def unpadded(blocks):
+            return blocks.reshape(9, BP, 768)[:, :BT].reshape(tokens.shape)
+
+        g_qkv, g_proj, g_fc1, g_fc2, out, dx, v0, v1, v2, v3, v4, v5, fc1b, qvb, relh, relw = whole_call(
+            padded(tokens), padded(out_grad), jnp.transpose(window_ids, (1, 0, 2)), jnp.transpose(qkv_weight, (1, 0, 2)),
+            proj_weight, fc1_weight, fc2_weight.T, vec, jnp.asarray(key_tail(), BF), tab,
+        )
+        v0, v1, v2, v3, v4, v5 = (v.reshape(768) for v in (v0, v1, v2, v3, v4, v5))
+        return (
+            unpadded(out), unpadded(dx).astype(F32), v4, v5, jnp.transpose(g_qkv, (1, 0, 2)), qvb, relh, relw, g_proj,
+            v2, v0, v1, g_fc1, fc1b.reshape(-1), g_fc2.T, v3,
+        )
+
     shard = jnp.stack(
         [
             jnp.concatenate([qkv_weight.reshape(-1, 576), proj_weight.T], axis=1),
@@ -994,15 +1095,12 @@
     tabt = (tab * BF(8)).T
     ktail = jnp.asarray(key_tail(), BF)
 
-    if links:
-        own, out, dx, vg, tg = whole_call(xh, coth, shard, small, mask, vec, ktail, fwd, back, tab, tabt)
-    else:
-        x, cot, whole = plain_gather(xh, coth, shard)
-        small = lax.all_gather(small, "tensor", axis=0)
-        out, gn, gh, grads, vg, tg = compute(
-            x, cot, mask, whole.reshape(3, 4, 768, 768), vec, small[:, 1:2, :576], small[:, 0:1], ktail, fwd, back, tab, tabt
-        )
-        own, out, dx, vg, tg = plain_scatter(grads, x, mask[:NR], vec, gn, gh, vg, tg, out)
+    x, cot, whole = plain_gather(xh, coth, shard)
+    small = lax.all_gather(small, "tensor", axis=0)
+    out, gn, gh, grads, vg, tg = compute(
+        x, cot, mask, whole.reshape(3, 4, 768, 768), vec, small[:, 1:2, :576], small[:, 0:1], ktail, fwd, back, tab, tabt
+    )
+    own, out, dx, vg, tg = plain_scatter(grads, x, mask[:NR], vec, gn, gh, vg, tg, out)
 
     def tokens_of(blocks):
         return blocks.reshape(9, BP, 768)[:, :BT].reshape(tokens.shape)

time: 238 us -> 215 us (0.903)
  local copies, waits for them, and re-layouts: 27.6 us -> 16.2 us
  between operations: 11.4 us -> 0.84 us
    another operation x10 -> x0, local copies, waits for them, and re-layouts: 5.01 us -> none  [the longest x7 4.16 us: per_device(): jnp.stack([norm1_gain, norm1_bias, proj_bias, norm2_gain, norm2_bias, fc2...]
    slice x6 -> x0, local copies, waits for them, and re-layouts: 3.83 us -> none  [the longest x1 1.62 us: per_device(): vg[3]]
    unnamed x40 -> x46, local copies, waits for them, and re-layouts: 5.27 us -> 8.82 us
    convert_element_type x4 -> x8, other arithmetic: 1.55 us -> 4.95 us  [the longest x7 4.84 us: per_device(): vec = jnp.where(row == n, v.astype(F32)[None, :], vec)]
    reshape x7 -> x4, local copies, waits for them, and re-layouts: 4.69 us -> 4.91 us  [the longest x1 2.22 us: unpadded(): return blocks.reshape(9, BP, 768)[:, :BT].reshape(tokens.shape)]
where the time goes in v3:
time: 215 us
  Pallas kernels  190 us (88%)
  local copies, waits for them, and re-layouts  16.2 us (8%)
  other arithmetic  7.69 us (4%)
    pallas_call x1, Pallas kernels, whole_call(): pl.pallas_call(whole_kernel, out_shape=(shp((3, 96, 192), F32), shp((192,...  190 us
    unnamed x46, local copies, waits for them, and re-layouts  8.82 us
    convert_element_type x7, other arithmetic, per_device(): vec = jnp.where(row == n, v.astype(F32)[None, :], vec)  4.84 us

profile of v3, /device:TPU:0, one launch (start us, length us, event | category | flops | bytes accessed | tf_op | source)
XLA Modules:
  0.0 214.8 jit_solution(15472095894681916080)
XLA Ops:
  0.7 0.7 convert_element_type.51
  1.4 0.7 convert_element_type.50
  2.1 0.7 convert_element_type.49
  2.8 0.7 convert_element_type.48
  3.5 0.7 convert_element_type.47
  4.2 0.7 convert_element_type.45
  4.9 0.7 convert_element_type.46
  5.5 1.4 select_select_fusion.vec_ref
  6.9 1.3 pad_add_fusion.tab_ref
  8.3 1.3 reshape.96
  9.7 1.3 pad_bitcast_fusion
  11.0 190.1 %shard_map.297 = (f32[3,96,192]{2,1,0:T(8,128)}, f32[192,96]{1,0:T(8,128)}, f32[96,768]{1,0:T(8,128)}, f32[96,768]{1,0:T(8,128)}, bf16[9,7,8,768]{3,2,1,0:T(8,12...) custom-call(bf16[9,7,8,768]{3,2,1,0:T(8,128)(2,1)} %get-tuple-elemen, ...), custom_call_target="tpu_custom_call" | custom-call | tf_op jit(solution)/shard_map/pallas_call | solution.py:968
  201.1 2.2 %reshape.101 = bf16[1,3,147,768]{3,2,1,0:T(8,128)(2,1)} reshape(bf16[9,49,768]{2,1,0:T(8,128)(2,1)} %bitcast.20) | data formatting | bytes 1354752 | tf_op jit(solution)/shard_map/reshape | solution.py:1047
  203.5 2.5 %reshape.110 = f32[1,3,147,768]{3,0,2,1:T(1,128)} reshape(f32[9,49,768]{2,1,0:T(8,128)S(1)} %slice_convert_fusion) | data formatting | bytes 2709504 | tf_op jit(solution)/shard_map/convert_element_type | solution.py:1055
  206.0 0.6 copy.48
  206.6 0.6 copy.49
  207.2 0.7 copy.50
  208.5 0.6 copy.52
  209.1 0.6 copy.53
  209.7 0.6 copy.54
  210.4 0.6 copy.55
  212.2 0.7 copy.58
  212.9 0.6 copy.59
  213.5 0.7 copy.60
  (42 shorter events, 2.7 us)
Async XLA Ops:
  0.6 8.9 %copy-start.1 = (bf16[1,3,147,768]{3,2,1,0:T(8,128)(2,1)S(1)}, bf16[1,3,147,768]{3,2,1,0:T(8,128)(2,1)}, u32[]{:S(2)}) copy-start(bf16[1,3,147,768]{3,2,1,0:T(8,128)(2,1)} %param.34) | copy-start | bytes 2032132
  201.0 2.2 %copy-start = (bf16[9,7,8,768]{3,2,1,0:T(8,128)(2,1)S(1)}, bf16[9,7,8,768]{3,2,1,0:T(8,128)(2,1)}, u32[]{:S(2)}) copy-start(bf16[9,7,8,768]{3,2,1,0:T(8,128)(2,1)} %get-tuple-element.33) | copy-start | bytes 2322436
  203.4 2.6 %copy-start.15 = (f32[6,128]{1,0:T(8,128)S(1)}, f32[6,128]{1,0:T(8,128)}, u32[]{:S(2)}) copy-start(f32[6,128]{1,0:T(8,128)} %get-tuple-element.34) | copy-start | bytes 9220
  203.4 3.2 %copy-start.14 = (f32[6,128]{1,0:T(8,128)S(1)}, f32[6,128]{1,0:T(8,128)}, u32[]{:S(2)}) copy-start(f32[6,128]{1,0:T(8,128)} %get-tuple-element.35) | copy-start | bytes 9220
  203.4 3.8 %copy-start.4 = (f32[3,96,192]{2,1,0:T(8,128)S(1)}, f32[3,96,192]{2,1,0:T(8,128)}, u32[]{:S(2)}) copy-start(f32[3,96,192]{2,1,0:T(8,128)} %get-tuple-element.36) | copy-start | bytes 663556
  203.4 4.5 %copy-start.9 = (f32[2,768]{1,0:T(2,128)S(1)}, f32[2,768]{1,0:T(2,128)}, u32[]{:S(2)}) copy-start(f32[2,768]{1,0:T(2,128)} %get-tuple-element.77) | copy-start | bytes 18436
  203.4 5.1 %copy-start.7 = (f32[27,64]{1,0:T(8,128)S(1)}, f32[27,64]{1,0:T(8,128)}, u32[]{:S(2)}) copy-start(f32[27,64]{1,0:T(8,128)} %get-tuple-element.78) | copy-start | bytes 20740
  203.4 5.7 %copy-start.6 = (f32[27,64]{1,0:T(8,128)S(1)}, f32[27,64]{1,0:T(8,128)}, u32[]{:S(2)}) copy-start(f32[27,64]{1,0:T(8,128)} %get-tuple-element.79) | copy-start | bytes 20740
  203.5 6.3 %copy-start.5 = (f32[192,96]{1,0:T(8,128)S(1)}, f32[192,96]{1,0:T(8,128)}, u32[]{:S(2)}) copy-start(f32[192,96]{1,0:T(8,128)} %get-tuple-element.80) | copy-start | bytes 221188
  203.5 6.9 %copy-start.13 = (f32[6,128]{1,0:T(8,128)S(1)}, f32[6,128]{1,0:T(8,128)}, u32[]{:S(2)}) copy-start(f32[6,128]{1,0:T(8,128)} %get-tuple-element.41) | copy-start | bytes 9220
  203.5 7.5 %copy-start.12 = (f32[6,128]{1,0:T(8,128)S(1)}, f32[6,128]{1,0:T(8,128)}, u32[]{:S(2)}) copy-start(f32[6,128]{1,0:T(8,128)} %get-tuple-element.42) | copy-start | bytes 9220
  203.5 8.1 %copy-start.11 = (f32[6,128]{1,0:T(8,128)S(1)}, f32[6,128]{1,0:T(8,128)}, u32[]{:S(2)}) copy-start(f32[6,128]{1,0:T(8,128)} %get-tuple-element.43) | copy-start | bytes 9220
  203.5 8.7 %copy-start.3 = (f32[96,768]{1,0:T(8,128)S(1)}, f32[96,768]{1,0:T(8,128)}, u32[]{:S(2)}) copy-start(f32[96,768]{1,0:T(8,128)} %get-tuple-element.84) | copy-start | bytes 884740
  203.5 9.4 %copy-start.8 = (f32[24,128]{1,0:T(8,128)S(1)}, f32[24,128]{1,0:T(8,128)}, u32[]{:S(2)}) copy-start(f32[24,128]{1,0:T(8,128)} %get-tuple-element.45) | copy-start | bytes 36868
  203.5 10.0 %copy-start.2 = (f32[96,768]{1,0:T(8,128)S(1)}, f32[96,768]{1,0:T(8,128)}, u32[]{:S(2)}) copy-start(f32[96,768]{1,0:T(8,128)} %get-tuple-element.46) | copy-start | bytes 884740
  206.0 8.2 %copy-start.10 = (f32[6,128]{1,0:T(8,128)S(1)}, f32[6,128]{1,0:T(8,128)}, u32[]{:S(2)}) copy-start(f32[6,128]{1,0:T(8,128)} %get-tuple-element.47) | copy-start | bytes 9220

commit v4 on v3

--- a/solution.py
+++ b/solution.py
@@ -620,10 +620,10 @@
 
 
 def whole_kernel(
-    x_in, cot_in, ids, qkv_w, proj_w, fc1_w, fc2_w, vec_ref, ktail_ref, tab_ref,
-    g_qkv, g_proj, g_fc1, g_fc2, out_h, dx_h, v0, v1, v2, v3, v4, v5, fc1b_out, qvb_out, relh_out, relw_out,
-    shard0, small, mask_ref, fwd_ref, back_ref,
-    w, r1, r2, r3, r4, x, cot, sm, ob, dx, gn, hid, gn2, gs, gsr, vg, tg, vr, tr,
+    x_raw, cot_raw, ids, qkv_w, proj_w, fc1_w, fc2_w, u0, u1, u2, u3, u4, u5, u6, qvb_in, relh_in, relw_in, ktail_ref,
+    own, out_h, dx_h, vg_out, tg_out,
+    shard0, small, mask_ref, fwd_ref, back_ref, vec_ref, tab_ref, tabf,
+    w, r1, r2, r3, r4, x, cot, sm, raw, dx, gn, hid, gn2, gs, gsr, vg, tg, vr, tr,
     nrm, proj, qaug, kaug, vals, probs, att, nr2, act, gup, gml, dqkv, send, recv, local,
 ):
     links = Links(send, recv)
@@ -631,7 +631,6 @@
     rows_of = Rows(links, local)
     ag = Gather(links, (shard0, fc1_w, fc2_w), w, local.at[pl.ds(40, 3)], AG0)
     rs = Scatter(links, w, r1, r2, r3, r4, RS0)
-    g1, b1, pb, g2, b2, fb = (vec_ref[i : i + 1, :] for i in range(6))
 
     def rank(order, m):
         i = jnp.int32(order[3])
@@ -684,37 +683,63 @@
         var = jnp.mean(c * c, axis=-1, keepdims=True)
         return c, lax.rsqrt(var + 1e-6)
 
+    read_x = pltpu.make_async_copy(x_raw, raw, local.at[44])
+    read_x.start()
     for t in range(3):
         shard0[:, 192 * t : 192 * t + 192] = qkv_w[t]
     shard0[:, 576:] = proj_w[...].astype(F32).T.astype(BF)
-    small[...] = jnp.zeros_like(small)
-    small[0:1, :] = vec_ref[6:7, :]
-    small[1:2, 0:192] = vec_ref[8:9, 0:192]
-    small[1:2, 384:576] = vec_ref[9:10, 0:192]
     x[63] = jnp.zeros((8, 768), BF)
     cot[63] = jnp.zeros((8, 768), BF)
     links.barrier()
     for b in (0, 1):
         ag.along(*BLOCKS[b])
+    small[...] = jnp.zeros_like(small)
+    for n, u in enumerate((u0, u1, u2, u3, u4, u5, u6)):
+        ref, row = (vec_ref, n) if n < 6 else (small, 0)
+        uf = u[...].astype(F32)
+        for c in range(6):
+            ref[row : row + 1, 128 * c : 128 * c + 128] = uf[c : c + 1, :]
+    qvb = qvb_in[...].astype(F32)
+    small[1:2, 0:192] = qvb[0:1]
+    small[1:2, 384:576] = qvb[1:2]
     bias = [links.copy(small, sm.at[z], BS + d - 1, links.zdev((z + d) % 4)) for d in (1, 2, 3)]
     keep_bias = pltpu.make_async_copy(small, sm.at[z], local.at[43])
     keep_bias.start()
     for c in bias:
         c.start()
-    rows_of.inward(x_in, x, X_SLOTS, XS, "start")
     ag.own_z(0)
-    rows_of.inward(cot_in, cot, range(9), CS, "start")
+
+    def pad_blocks(held):
+        for m in range(3):
+            gn2[0:147, :] = raw[m].astype(F32)
+            for b in range(3):
+                v = gn2[BT * b : BT * b + BP, :]
+                v = jnp.where(lax.broadcasted_iota(jnp.int32, v.shape, 0) < BT, v, 0.0)
+                held[3 * m + b] = v.astype(BF).reshape(7, 8, 768)
+
+    held = dx.at[pl.ds(0, 63)].reshape(9, 7, 8, 768)
+    read_x.wait()
+    pad_blocks(held)
+    rows_of.inward(held, x, X_SLOTS, XS, "start")
+    read_cot = pltpu.make_async_copy(cot_raw, raw, local.at[44])
+    read_cot.start()
     ag.own_z(1)
+    tabf[...] = jnp.zeros_like(tabf)
+    tabf[0:27, :] = relh_in[...].astype(F32)
+    tabf[32:59, :] = relw_in[...].astype(F32)
+    tab_ref[...] = tabf[...].astype(BF)
 
     vg[...] = jnp.zeros_like(vg)
     tg[...] = jnp.zeros_like(tg)
     fill_tables(z, ids, mask_ref, fwd_ref, back_ref)
-    rows_of.inward(x_in, x, X_SLOTS, XS, "wait")
+    rows_of.inward(held, x, X_SLOTS, XS, "wait")
     x[56:63] = x[pl.ds(NR // 8 + 7 * z, 7)]
     for c in bias:
         c.wait_recv()
     keep_bias.wait()
 
+    g1, b1, pb, g2, b2, fb = (vec_ref[i : i + 1, :] for i in range(6))
+
     for r0 in range(0, NE, 32):
         rows = slice(r0, r0 + 32)
         c, rstd = stats(x[r0 // 8 : r0 // 8 + 4].astype(F32).reshape(32, 768))
@@ -723,6 +748,10 @@
     ag.across(*BLOCKS[0])
     tick(0)
     ag.own_z(2)
+    rows_of.inward(held, x, X_SLOTS, XS, "drain")
+    read_cot.wait()
+    pad_blocks(held)
+    rows_of.inward(held, cot, range(9), CS, "start")
     mix = gn.at[pl.ds(0, NR)]
     mix[...] = jnp.zeros_like(mix)
 
@@ -763,7 +792,7 @@
         return 0
 
     lax.fori_loop(0, 4, fwd_t, 0)
-    rows_of.inward(cot_in, cot, range(9), CS, "wait")
+    rows_of.inward(held, cot, range(9), CS, "wait")
     now("L")
 
     for r0 in range(0, NR, 32):
@@ -813,10 +842,12 @@
         return jnp.sum(v.reshape(4, 8, 768), axis=0)
 
     gbl = act
+    rows_of.inward(held, cot, range(9), CS, "drain")
+    ob = cot
     for r0 in range(0, NR, 32):
         rows = slice(r0, r0 + 32)
         mk = mask_ref[rows, :]
-        gm = mk * cot[r0 // 8 : r0 // 8 + 4].astype(F32).reshape(32, 768)
+        gm = gml[rows, :].astype(F32)
         hv = hid[rows, :]
         ob[r0 // 8 : r0 // 8 + 4] = (mk * (hv + mix[rows, :] + fb)).reshape(4, 8, 768).astype(BF)
         c, rstd = stats(hv)
@@ -885,28 +916,14 @@
     now("T2")
     small_sums(links, vg, tg, vr, tr, now)
     now("T3")
-    for n, ref in enumerate((v0, v1, v2, v3, v4, v5)):
-        for c in range(6):
-            ref[c : c + 1, :] = vg[5, n : n + 1, 128 * c : 128 * c + 128]
-    for t in range(4):
-        for c in range(6):
-            fc1b_out[6 * t + c : 6 * t + c + 1, :] = vg[5, 8 + t : 9 + t, 128 * c : 128 * c + 128]
-        qvb_out[0:1, 192 * t : 192 * t + 192] = vg[5, 12 + t : 13 + t, 0:192]
-        qvb_out[1:2, 192 * t : 192 * t + 192] = vg[5, 12 + t : 13 + t, 384:576]
-    relh_out[...] = tg[5, 0:27, :64] * 8.0
-    relw_out[...] = tg[5, 32:59, :64] * 8.0
-    g_fc2[...] = rs.total(2)
-    g_fc1[...] = rs.total(1)
-    fin = rs.total(0)
-    for t in range(3):
-        g_qkv[t] = fin[:, 192 * t : 192 * t + 192]
-    g_proj[...] = fin[:, 576:].T
+    vg_out[...] = vg[5]
+    tg_out[...] = tg[5]
+    for k in (2, 1, 0):
+        own[k] = rs.total(k)
     rows_of.outward(ob, out_h, RET0, 22, "wait")
     rows_of.outward(dx, dx_h, DX0, 31, "wait")
     rows_of.outward(ob, out_h, RET0, 22, "drain")
     rows_of.outward(dx, dx_h, DX0, 31, "drain")
-    rows_of.inward(x_in, x, X_SLOTS, XS, "drain")
-    rows_of.inward(cot_in, cot, range(9), CS, "drain")
     for c in sh + bias:
         c.wait_send()
     for k in range(3):
@@ -959,7 +976,49 @@
         c.wait_send()
 
 
-def whole_call(xh, coth, ids, qkv_w, proj_w, fc1_w, fc2_w, vec, ktail, tab):
+def final_kernel(
+    own, out_h, dx_h, vg, tg, out, dx, g_qkv, g_proj, g_fc1, g_fc2, v0, v1, v2, v3, v4, v5, fc1b_out, qvb_out, relh_out, relw_out,
+    rows,
+):
+    for m in range(3):
+        for b in range(3):
+            dx[m, BT * b : BT * b + BT, :] = dx_h[3 * m + b].astype(F32).reshape(BP, 768)[:BT]
+            rows[BT * b : BT * b + BT, :] = out_h[3 * m + b].astype(F32).reshape(BP, 768)[:BT]
+        out[m] = rows[...].astype(BF)
+    for n, ref in enumerate((v0, v1, v2, v3, v4, v5)):
+        for c in range(6):
+            ref[c : c + 1, :] = vg[n : n + 1, 128 * c : 128 * c + 128]
+    for t in range(4):
+        for c in range(6):
+            fc1b_out[6 * t + c : 6 * t + c + 1, :] = vg[8 + t : 9 + t, 128 * c : 128 * c + 128]
+        qvb_out[0:1, 192 * t : 192 * t + 192] = vg[12 + t : 13 + t, 0:192]
+        qvb_out[1:2, 192 * t : 192 * t + 192] = vg[12 + t : 13 + t, 384:576]
+    relh_out[...] = tg[0:27, :64] * 8.0
+    relw_out[...] = tg[32:59, :64] * 8.0
+    for t in range(3):
+        g_qkv[t] = own[0, :, 192 * t : 192 * t + 192]
+    g_proj[...] = own[0, :, 576:].T
+    g_fc1[...] = own[1]
+    g_fc2[...] = own[2]
+
+
+def final_call(*arrays):
+    shp = jax.ShapeDtypeStruct
+    vm = pl.BlockSpec(memory_space=pltpu.VMEM)
+    return pl.pallas_call(
+        final_kernel,
+        out_shape=(
+            shp((3, 147, 768), BF), shp((3, 147, 768), F32), shp((3, 96, 192), F32), shp((192, 96), F32), shp((96, 768), F32),
+            shp((96, 768), F32), *[shp((6, 128), F32)] * 6, shp((24, 128), F32), shp((2, 768), F32), shp((27, 64), F32),
+            shp((27, 64), F32),
+        ),
+        in_specs=[vm] * 5,
+        out_specs=(vm,) * 16,
+        scratch_shapes=[pltpu.VMEM((147, 768), F32)],
+    )(*arrays)
+
+
+def whole_call(*arrays):
     shp = jax.ShapeDtypeStruct
     vm = pl.BlockSpec(memory_space=pltpu.VMEM)
     hbm = pl.BlockSpec(memory_space=pl.ANY)
@@ -968,17 +1027,16 @@
     return pl.pallas_call(
         whole_kernel,
         out_shape=(
-            shp((3, 96, 192), F32), shp((192, 96), F32), shp((96, 768), F32), shp((96, 768), F32),
-            shp((9, 7, 8, 768), BF), shp((9, 7, 8, 768), BF), *[shp((6, 128), F32)] * 6, shp((24, 128), F32),
-            shp((2, 768), F32), shp((27, 64), F32), shp((27, 64), F32),
+            shp((3, 96, 768), F32), shp((9, 7, 8, 768), BF), shp((9, 7, 8, 768), BF), shp((16, 768), F32), shp((64, 128), F32),
         ),
-        in_specs=[hbm, hbm, pl.BlockSpec(memory_space=pltpu.SMEM)] + [vm] * 7,
-        out_specs=(vm, vm, vm, vm, hbm, hbm) + (vm,) * 10,
+        in_specs=[hbm, hbm, pl.BlockSpec(memory_space=pltpu.SMEM)] + [vm] * 15,
+        out_specs=(vm, hbm, hbm, vm, vm),
         scratch_shapes=[
             V((96, 768), BF), V((8, 768), F32), V((NE, 1), F32), V((NR, 128), jnp.int32), V((NR, 128), jnp.int32),
+            V((8, 768), F32), V((128, 64), BF), V((128, 64), F32),
             V((3, 4, 2, 2, 2, 96, 768), BF), V((12, 2, 2, 96, 768), BF), V((12, 2, 2, 48, 768), BF), V((12, 2, 48, 768), BF),
             V((3, 3, 96, 768), BF), V((NE // 8, 8, 768), BF), V((NR // 8, 8, 768), BF), V((4, 8, 768), F32),
-            V((NR // 8, 8, 768), BF), V((NR // 8, 8, 768), BF), V((NE, 768), F32), V((NR, 768), F32), V((NR, 768), F32),
+            V((3, 147, 768), BF), V((NR // 8, 8, 768), BF), V((NE, 768), F32), V((NR, 768), F32), V((NR, 768), F32),
             V((WR // 8, 8, 768), BF), V((3, 7, 8, 768), BF), V((6, 16, 768), F32), V((6, 64, 128), F32),
             V((5, 16, 768), F32), V((5, 64, 128), F32),
             V((NE, 768), BF), V((NE, 576), F32), V((HEADS, NR, 128), BF), V((HEADS, 3, WR, 128), BF), V((HEADS, 3, WR, 64), BF),
@@ -986,7 +1044,7 @@
             V((NE, 576), BF), dma((SEMS,)), dma((SEMS,)), dma((48,)),
         ],
         compiler_params=pltpu.CompilerParams(collective_id=0, has_side_effects=True, vmem_limit_bytes=67043328),
-    )(xh, coth, ids, qkv_w, proj_w, fc1_w, fc2_w, vec, ktail, tab)
+    )(*arrays)
 
 
 def plain_gather(xh, coth, shard):
@@ -1034,26 +1092,16 @@
 
     if links:
         vectors = (norm1_gain, norm1_bias, proj_bias, norm2_gain, norm2_bias, fc2_bias, fc1_bias)
-        row = lax.broadcasted_iota(jnp.int32, (16, 768), 0)
-        vec = jnp.pad(qv_bias.astype(F32), ((8, 6), (0, 576)))
-        for n, v in enumerate(vectors):
-            vec = jnp.where(row == n, v.astype(F32)[None, :], vec)
-        tab = jnp.pad(rel_height, ((0, 101), (0, 0))) + jnp.pad(rel_width, ((32, 69), (0, 0)))
-
-        def padded(rows):
-            return jnp.pad(rows.reshape(9, BT, 768), ((0, 0), (0, BP - BT), (0, 0))).reshape(9, 7, 8, 768)
-
-        def unpadded(blocks):
-            return blocks.reshape(9, BP, 768)[:, :BT].reshape(tokens.shape)
-
-        g_qkv, g_proj, g_fc1, g_fc2, out, dx, v0, v1, v2, v3, v4, v5, fc1b, qvb, relh, relw = whole_call(
-            padded(tokens), padded(out_grad), jnp.transpose(window_ids, (1, 0, 2)), jnp.transpose(qkv_weight, (1, 0, 2)),
-            proj_weight, fc1_weight, fc2_weight.T, vec, jnp.asarray(key_tail(), BF), tab,
+        done = whole_call(
+            tokens[0], out_grad[0], jnp.transpose(window_ids, (1, 0, 2)), jnp.transpose(qkv_weight, (1, 0, 2)), proj_weight,
+            fc1_weight, fc2_weight.T, *(v.reshape(6, 128) for v in vectors), qv_bias, rel_height, rel_width,
+            jnp.asarray(key_tail(), BF),
         )
+        out, dx, g_qkv, g_proj, g_fc1, g_fc2, v0, v1, v2, v3, v4, v5, fc1b, qvb, relh, relw = final_call(*done)
         v0, v1, v2, v3, v4, v5 = (v.reshape(768) for v in (v0, v1, v2, v3, v4, v5))
         return (
-            unpadded(out), unpadded(dx).astype(F32), v4, v5, jnp.transpose(g_qkv, (1, 0, 2)), qvb, relh, relw, g_proj,
-            v2, v0, v1, g_fc1, fc1b.reshape(-1), g_fc2.T, v3,
+            out[None], dx[None], v4, v5, jnp.transpose(g_qkv, (1, 0, 2)), qvb, relh, relw, g_proj, v2, v0, v1, g_fc1,
+            fc1b.reshape(-1), g_fc2.T, v3,
         )
 
     shard = jnp.stack(

time: 215 us -> 211 us (0.981)
  Pallas kernels: 190 us -> 206 us
  local copies, waits for them, and re-layouts: 16.2 us -> 3.81 us
  other arithmetic: 7.69 us -> 0 us
    pallas_call x1 -> x2, Pallas kernels: 190 us -> 206 us  [the longest x1 203 us: whole_call(): pl.pallas_call(whole_kernel, out_shape=(shp((3, 96, 768), F32), shp((9, 7...]
    unnamed x46 -> x1, local copies, waits for them, and re-layouts: 8.82 us -> 3.81 us
    convert_element_type x8 -> x0, other arithmetic: 4.95 us -> none  [the longest x7 4.84 us: per_device(): vec = jnp.where(row == n, v.astype(F32)[None, :], vec)]
    reshape x4 -> x0, local copies, waits for them, and re-layouts: 4.91 us -> none  [the longest x1 2.22 us: unpadded(): return blocks.reshape(9, BP, 768)[:, :BT].reshape(tokens.shape)]
    convert_element_type x1 -> x0, local copies, waits for them, and re-layouts: 2.48 us -> none  [per_device(): unpadded(dx).astype(F32)]
where the time goes in v4:
time: 211 us
  Pallas kernels  206 us (98%)
  local copies, waits for them, and re-layouts  3.81 us (2%)
    pallas_call x1, Pallas kernels, whole_call(): pl.pallas_call(whole_kernel, out_shape=(shp((3, 96, 768), F32), shp((9, 7...  203 us

profile of v4, /device:TPU:0, one launch (start us, length us, event | category | flops | bytes accessed | tf_op | source)
XLA Modules:
  0.0 210.6 jit_solution(14816601550208480645)
XLA Ops:
  0.7 202.6 %shard_map.297 = (f32[3,96,768]{2,1,0:T(8,128)}, bf16[9,7,8,768]{3,2,1,0:T(8,128)(2,1)}, bf16[9,7,8,768]{3,2,1,0:T(8,128)(2,1)}, f32[16,768]{1,0:T(8,128)}, f32[64,128]{1,0:T(8,128)}) custom-call(bf16[3,147,768]{2,1,0:T(8,128)(2,1)} %bitcast.24, bf16[3,147,768]{2,1,0:T(8,128)(2,1)} %bitcast.25, s32[3,1,3]{2,1,0:T(1,128)} %bitcast.35, ...), custom_call_target="tpu_custom_call" | custom-call | tf_op jit(solution)/shard_map/pallas_call | solution.py:1027
  203.3 3.5 %shard_map.298 = (bf16[3,147,768]{2,1,0:T(8,128)(2,1)}, f32[3,147,768]{2,1,0:T(8,128)}, f32[3,96,192]{2,1,0:T(8,128)}, f32[192,96]{1,0:T(8,128)}, f32[96,768]{1,...) custom-call(f32[3,96,768]{2,1,0:T(8,128)} %get-tuple-element.37.own,, ...), custom_call_target="tpu_custom_call" | custom-call | tf_op jit(solution)/shard_map/pallas_call | solution.py:1008
  206.8 3.8 %copy.34 = f32[1,3,147,768]{3,0,2,1:T(1,128)} copy(f32[1,3,147,768]{3,2,1,0:T(8,128)} %bitcast.23) | data formatting | bytes 2709504

commit v5 on v4

--- a/solution.py
+++ b/solution.py
@@ -541,9 +541,9 @@
     [("M", n, j) for n in range(4) for j in range(5)] + ["N"] + [("B", n, j) for n in range(4) for j in range(3)]
     + ["T0", "T1", "T2", "S0", "S1", "S2", "S3", "S4", "T3"]
 )
-TICKS = {1: ("F", 0, 0), 2: ("F", 0, 2), 3: ("F", 1, 1), 4: ("F", 2, 1), 5: ("F", 3, 1), 6: "L", 7: ("M", 0, 0), 8: ("M", 0, 4),
+TICKS = {1: ("F", 0, 0), 2: ("F", 0, 3), 3: ("F", 1, 2), 4: ("F", 2, 2), 5: ("F", 3, 2), 6: "L", 7: ("M", 0, 0), 8: ("M", 0, 4),
          9: ("M", 1, 1), 10: ("M", 1, 4), 11: ("M", 2, 1)}
-MLP_LAGS = ((0, 6, 11), (1, 8, 12))
+MLP_LAGS = ((1, 9, 15), (3, 11, 17))
 BWD_LAGS = (0, 3, 5)
 
 
@@ -620,12 +620,15 @@
 
 
 def whole_kernel(
-    x_raw, cot_raw, ids, qkv_w, proj_w, fc1_w, fc2_w, u0, u1, u2, u3, u4, u5, u6, qvb_in, relh_in, relw_in, ktail_ref,
-    own, out_h, dx_h, vg_out, tg_out,
-    shard0, small, mask_ref, fwd_ref, back_ref, vec_ref, tab_ref, tabf,
-    w, r1, r2, r3, r4, x, cot, sm, raw, dx, gn, hid, gn2, gs, gsr, vg, tg, vr, tr,
-    nrm, proj, qaug, kaug, vals, probs, att, nr2, act, gup, gml, dqkv, send, recv, local,
+    x_raw, cot_raw, ids, *refs,
 ):
+    given, refs, held_in, load = refs[:15], refs[15:-16], refs[-16:-1], refs[-1]
+    qkv_w, proj_w, fc1_w, fc2_w, u0, u1, u2, u3, u4, u5, u6, qvb_in, relh_in, relw_in, ktail_ref = held_in
+    (
+        own, out_h, dx_h, vg_out, tg_out, shard0, small, mask_ref, fwd_ref, back_ref, vec_ref, tab_ref, tabf, w, r1,
+        r2, r3, r4, x, cot, sm, raw, dx, gn, hid, gn2, gs, gsr, vg, tg, vr, tr, nrm, proj, qaug, kaug, vals, probs,
+        att, nr2, act, gup, gml, dqkv, send, recv, local,
+    ) = refs
     links = Links(send, recv)
     z = links.z
     rows_of = Rows(links, local)
@@ -685,12 +688,19 @@
 
     read_x = pltpu.make_async_copy(x_raw, raw, local.at[44])
     read_x.start()
+    loads = [pltpu.make_async_copy(a, b, load.at[n]) for n, (a, b) in enumerate(zip(given, held_in))]
+    for c in loads:
+        c.start()
+    loads[0].wait()
+    loads[1].wait()
     for t in range(3):
         shard0[:, 192 * t : 192 * t + 192] = qkv_w[t]
     shard0[:, 576:] = proj_w[...].astype(F32).T.astype(BF)
     x[63] = jnp.zeros((8, 768), BF)
     cot[63] = jnp.zeros((8, 768), BF)
     links.barrier()
+    for c in loads[2:]:
+        c.wait()
     for b in (0, 1):
         ag.along(*BLOCKS[b])
     small[...] = jnp.zeros_like(small)
@@ -707,7 +717,6 @@
     keep_bias.start()
     for c in bias:
         c.start()
-    ag.own_z(0)
 
     def pad_blocks(held):
         for m in range(3):
@@ -721,6 +730,7 @@
     read_x.wait()
     pad_blocks(held)
     rows_of.inward(held, x, X_SLOTS, XS, "start")
+    ag.own_z(0)
     read_cot = pltpu.make_async_copy(cot_raw, raw, local.at[44])
     read_cot.start()
     ag.own_z(1)
@@ -785,10 +795,10 @@
                 p = (e * (1.0 / jnp.sum(e, axis=-1, keepdims=True))).astype(BF)
                 probs[hh, rows, :] = p
                 att[t, rows, 64 * h : 64 * h + 64] = dotf(p, vals[hh, wn], NN).astype(BF)
-            if h == 1:
-                hook(m, "F", 1)
+            if h < 2:
+                hook(m, "F", 1 + h)
         mix[...] += dotf(att[t], weight(0, t)[:, 576:], NT)
-        hook(m, "F", 2)
+        hook(m, "F", 3)
         return 0
 
     lax.fori_loop(0, 4, fwd_t, 0)
@@ -982,7 +992,8 @@
 ):
     for m in range(3):
         for b in range(3):
-            dx[m, BT * b : BT * b + BT, :] = dx_h[3 * m + b].astype(F32).reshape(BP, 768)[:BT]
+            n = BT * (3 * m + b)
+            dx[n : n + BT, 0, :] = dx_h[3 * m + b].astype(F32).reshape(BP, 768)[:BT]
             rows[BT * b : BT * b + BT, :] = out_h[3 * m + b].astype(F32).reshape(BP, 768)[:BT]
         out[m] = rows[...].astype(BF)
     for n, ref in enumerate((v0, v1, v2, v3, v4, v5)):
@@ -1008,7 +1019,7 @@
     return pl.pallas_call(
         final_kernel,
         out_shape=(
-            shp((3, 147, 768), BF), shp((3, 147, 768), F32), shp((3, 96, 192), F32), shp((192, 96), F32), shp((96, 768), F32),
+            shp((3, 147, 768), BF), shp((441, 1, 768), F32), shp((3, 96, 192), F32), shp((192, 96), F32), shp((96, 768), F32),
             shp((96, 768), F32), *[shp((6, 128), F32)] * 6, shp((24, 128), F32), shp((2, 768), F32), shp((27, 64), F32),
             shp((27, 64), F32),
         ),
@@ -1029,7 +1040,7 @@
         out_shape=(
             shp((3, 96, 768), F32), shp((9, 7, 8, 768), BF), shp((9, 7, 8, 768), BF), shp((16, 768), F32), shp((64, 128), F32),
         ),
-        in_specs=[hbm, hbm, pl.BlockSpec(memory_space=pltpu.SMEM)] + [vm] * 15,
+        in_specs=[hbm, hbm, pl.BlockSpec(memory_space=pltpu.SMEM)] + [hbm] * 15,
         out_specs=(vm, hbm, hbm, vm, vm),
         scratch_shapes=[
             V((96, 768), BF), V((8, 768), F32), V((NE, 1), F32), V((NR, 128), jnp.int32), V((NR, 128), jnp.int32),
@@ -1042,6 +1053,7 @@
             V((NE, 768), BF), V((NE, 576), F32), V((HEADS, NR, 128), BF), V((HEADS, 3, WR, 128), BF), V((HEADS, 3, WR, 64), BF),
             V((HEADS, NR, WR), BF), V((4, NR, 192), BF), V((NR, 768), BF), V((NR, 768), BF), V((NR, 768), BF), V((NR, 768), BF),
             V((NE, 576), BF), dma((SEMS,)), dma((SEMS,)), dma((48,)),
+            *[V(a.shape, a.dtype) for a in arrays[3:]], dma((15,)),
         ],
         compiler_params=pltpu.CompilerParams(collective_id=0, has_side_effects=True, vmem_limit_bytes=67043328),
     )(*arrays)
@@ -1100,7 +1112,7 @@
         out, dx, g_qkv, g_proj, g_fc1, g_fc2, v0, v1, v2, v3, v4, v5, fc1b, qvb, relh, relw = final_call(*done)
         v0, v1, v2, v3, v4, v5 = (v.reshape(768) for v in (v0, v1, v2, v3, v4, v5))
         return (
-            out[None], dx[None], v4, v5, jnp.transpose(g_qkv, (1, 0, 2)), qvb, relh, relw, g_proj, v2, v0, v1, g_fc1,
+            out[None], dx.reshape(1, 3, 147, 768), v4, v5, jnp.transpose(g_qkv, (1, 0, 2)), qvb, relh, relw, g_proj, v2, v0, v1, g_fc1,
             fc1b.reshape(-1), g_fc2.T, v3,
         )
 

time: 211 us -> 195 us (0.924)
  Pallas kernels: 206 us -> 194 us
  local copies, waits for them, and re-layouts: 3.81 us -> 0 us
    pallas_call x1, Pallas kernels: 203 us -> 190 us  [whole_call(): pl.pallas_call(whole_kernel, out_shape=(shp((3, 96, 768), F32), shp((9, 7...]
    unnamed x1 -> x0, local copies, waits for them, and re-layouts: 3.81 us -> none
where the time goes in v5:
time: 195 us
  Pallas kernels  194 us (99%)
    pallas_call x1, Pallas kernels, whole_call(): pl.pallas_call(whole_kernel, out_shape=(shp((3, 96, 768), F32), shp((9, 7...  190 us

profile of v5, /device:TPU:0, one launch (start us, length us, event | category | flops | bytes accessed | tf_op | source)
XLA Modules:
  0.0 195.0 jit_solution(1303366288866178557)
XLA Ops:
  0.7 190.5 %shard_map.297 = (f32[3,96,768]{2,1,0:T(8,128)}, bf16[9,7,8,768]{3,2,1,0:T(8,128)(2,1)}, bf16[9,7,8,768]{3,2,1,0:T(8,128)(2,1)}, f32[16,768]{1,0:T(8,128)}, f32[64,128]{1,0:T(8,128)}) custom-call(bf16[3,147,768]{2,1,0:T(8,128)(2,1)} %bitcast.23, bf16[3,147,768]{2,1,0:T(8,128)(2,1)} %bitcast.24, s32[3,1,3]{2,1,0:T(1,128)} %bitcast.34, ...), custom_call_target="tpu_custom_call" | custom-call | tf_op jit(solution)/shard_map/pallas_call | solution.py:1038
  191.1 3.7 %shard_map.298 = (bf16[3,147,768]{2,1,0:T(8,128)(2,1)}, f32[441,1,768]{2,1,0:T(1,128)}, f32[3,96,192]{2,1,0:T(8,128)}, f32[192,96]{1,0:T(8,128)}, f32[96,768]{1,...) custom-call(f32[3,96,768]{2,1,0:T(8,128)} %get-tuple-element.37.own,, ...), custom_call_target="tpu_custom_call" | custom-call | tf_op jit(solution)/shard_map/pallas_call | solution.py:1019

commit v6 on v5

--- a/solution.py
+++ b/solution.py
@@ -698,7 +698,19 @@
     shard0[:, 576:] = proj_w[...].astype(F32).T.astype(BF)
     x[63] = jnp.zeros((8, 768), BF)
     cot[63] = jnp.zeros((8, 768), BF)
+    def pad_blocks(held):
+        for m in range(3):
+            gn2[0:147, :] = raw[m].astype(F32)
+            for b in range(3):
+                v = gn2[BT * b : BT * b + BP, :]
+                v = jnp.where(lax.broadcasted_iota(jnp.int32, v.shape, 0) < BT, v, 0.0)
+                held[3 * m + b] = v.astype(BF).reshape(7, 8, 768)
+
+    held = dx.at[pl.ds(0, 63)].reshape(9, 7, 8, 768)
+    read_x.wait()
+    pad_blocks(held)
     links.barrier()
+    rows_of.inward(held, x, X_SLOTS, XS, "start")
     for c in loads[2:]:
         c.wait()
     for b in (0, 1):
@@ -718,18 +730,6 @@
     for c in bias:
         c.start()
 
-    def pad_blocks(held):
-        for m in range(3):
-            gn2[0:147, :] = raw[m].astype(F32)
-            for b in range(3):
-                v = gn2[BT * b : BT * b + BP, :]
-                v = jnp.where(lax.broadcasted_iota(jnp.int32, v.shape, 0) < BT, v, 0.0)
-                held[3 * m + b] = v.astype(BF).reshape(7, 8, 768)
-
-    held = dx.at[pl.ds(0, 63)].reshape(9, 7, 8, 768)
-    read_x.wait()
-    pad_blocks(held)
-    rows_of.inward(held, x, X_SLOTS, XS, "start")
     ag.own_z(0)
     read_cot = pltpu.make_async_copy(cot_raw, raw, local.at[44])
     read_cot.start()

time: 195 us -> 196 us (level)
  no operation moved by 1% of the time
where the time goes in v6:
time: 196 us
  Pallas kernels  195 us (99%)
    pallas_call x1, Pallas kernels, whole_call(): pl.pallas_call(whole_kernel, out_shape=(shp((3, 96, 768), F32), shp((9, 7...  191 us

profile of v6, /device:TPU:0, one launch (start us, length us, event | category | flops | bytes accessed | tf_op | source)
XLA Modules:
  0.0 195.8 jit_solution(6950925522768582389)
XLA Ops:
  0.7 191.3 %shard_map.297 = (f32[3,96,768]{2,1,0:T(8,128)}, bf16[9,7,8,768]{3,2,1,0:T(8,128)(2,1)}, bf16[9,7,8,768]{3,2,1,0:T(8,128)(2,1)}, f32[16,768]{1,0:T(8,128)}, f32[64,128]{1,0:T(8,128)}) custom-call(bf16[3,147,768]{2,1,0:T(8,128)(2,1)} %bitcast.23, bf16[3,147,768]{2,1,0:T(8,128)(2,1)} %bitcast.24, s32[3,1,3]{2,1,0:T(1,128)} %bitcast.34, ...), custom_call_target="tpu_custom_call" | custom-call | tf_op jit(solution)/shard_map/pallas_call | solution.py:1038
  192.0 3.7 %shard_map.298 = (bf16[3,147,768]{2,1,0:T(8,128)(2,1)}, f32[441,1,768]{2,1,0:T(1,128)}, f32[3,96,192]{2,1,0:T(8,128)}, f32[192,96]{1,0:T(8,128)}, f32[96,768]{1,...) custom-call(f32[3,96,768]{2,1,0:T(8,128)} %get-tuple-element.37.own,, ...), custom_call_target="tpu_custom_call" | custom-call | tf_op jit(solution)/shard_map/pallas_call | solution.py:1019
